TPU v7x, 128 devices: a whole 4x4x4 slice. The times are simulated.
128 devices in a mesh: group: 8 (over y_hi, x), fsdp: 16 (over z, y_lo, core).
Axes of the slice: x: 4, y: 4 (y_hi: 2, y_lo: 2; y = y_hi * 2 + y_lo), z: 4, core: 2. Of those that a mesh axis runs over, the one named last changes fastest.
Arguments:
- tokens_in: bfloat16 [131072, 2048], P(('group', 'fsdp')), may hold values from -6 to 6
- out_grad: bfloat16 [131072, 2048], P(('group', 'fsdp')), may hold values from -0.59765625 to 0.59765625
- w_in: bfloat16 [8, 2048, 8192], P('group', None, 'fsdp'), may hold values from -0.125 to 0.125
- w_out: bfloat16 [8, 8192, 2048], P('group', 'fsdp'), may hold values from -0.0625 to 0.0625
- chosen: int32 [128, 8, 16], P(('group', 'fsdp')), may hold values from 0 to 1023, as said below
- counts: int32 [128, 8], P(('group', 'fsdp')), may hold values from 1 to 16, as said below
- gates: float32 [128, 8, 16], P(('group', 'fsdp')), may hold values from 0.05 to 1
Outputs:
- grad_in: bfloat16 [131072, 2048], P(('group', 'fsdp'))
- grad_w_in: float32 [8, 2048, 8192], P('group', None, 'fsdp')
- grad_w_out: float32 [8, 8192, 2048], P('group', 'fsdp')
Inputs may be any that keep to these rules, and one draw needn't show every extreme that they name: `chosen`: the 16 slots of one image and one expert name distinct positions. `counts`: each image fills all 16 slots of at least one expert.
All inputs are finite; a program needn't handle non-finite values.
Results may differ from a plain program's by a relative error of at most 0.0057.
Values may be sent and summed in bfloat16 or wider, within the bound.
A program may use at most 128 MiB of HBM per device.

v0:
```python
import jax
import jax.numpy as jnp
from jax import lax
from jax.sharding import PartitionSpec as P

gelu_coef = 0.7978845608028654


def gelu_parts(hidden):
    inner_arg = gelu_coef * (hidden + 0.044715 * hidden * hidden * hidden)
    tangent = jnp.tanh(inner_arg)
    activation = 0.5 * hidden * (1.0 + tangent)
    slope = 0.5 * (1.0 + tangent) + 0.5 * hidden * (1.0 - tangent * tangent) * gelu_coef * (
        1.0 + 3.0 * 0.044715 * hidden * hidden
    )
    return (activation, slope)


def shards(tokens_in, out_grad, w_in, w_out, chosen, counts, gates):
    group_count = lax.axis_size("group")
    exp_local = w_in.shape[0]
    slot_count = chosen.shape[2]
    model_width = tokens_in.shape[1]
    slot_rows = chosen[0].reshape(-1)
    slot_iota = lax.broadcasted_iota(jnp.int32, chosen.shape[1:], 1)
    live_gate = jnp.where(slot_iota < counts[0][:, None], gates[0], jnp.float32(0.0))
    block_shape = (group_count, exp_local, slot_count, model_width)
    picked_x = jnp.take(tokens_in, slot_rows, axis=0).reshape(block_shape)
    picked_grad = (
        (live_gate.reshape(-1)[:, None] * jnp.take(out_grad, slot_rows, axis=0).astype(jnp.float32))
        .astype(jnp.bfloat16)
        .reshape(block_shape)
    )
    near_x, near_grad = (
        lax.all_to_all(picked_x, "group", split_axis=0, concat_axis=0, tiled=True),
        lax.all_to_all(picked_grad, "group", split_axis=0, concat_axis=0, tiled=True),
    )
    rows_x, rows_grad = (
        lax.all_gather(near_x, "fsdp", axis=0, tiled=True),
        lax.all_gather(near_grad, "fsdp", axis=0, tiled=True),
    )
    sources = rows_x.shape[0]
    expert_x = rows_x[:, 0].reshape(-1, model_width)
    expert_grad = rows_grad[:, 0].reshape(-1, model_width)
    hidden = jnp.dot(expert_x, w_in[0], preferred_element_type=jnp.float32)
    activation, gelu_slope = gelu_parts(hidden)
    activation = activation.astype(jnp.bfloat16)
    back_hidden = lax.dot_general(
        expert_grad, w_out[0], (((1,), (1,)), ((), ())), preferred_element_type=jnp.float32
    )
    hidden_grad = (back_hidden * gelu_slope).astype(jnp.bfloat16)
    grads_in_w = [
        lax.dot_general(
            expert_x, hidden_grad, (((0,), (0,)), ((), ())), preferred_element_type=jnp.float32
        )
    ]
    grads_out_w = [
        lax.dot_general(
            activation, expert_grad, (((0,), (0,)), ((), ())), preferred_element_type=jnp.float32
        )
    ]
    hidden_grads = [hidden_grad.reshape(sources, slot_count, -1)]
    stacked_grad = jnp.stack(hidden_grads, axis=1)
    term = jnp.einsum("secf,edf->secd", stacked_grad, w_in, preferred_element_type=jnp.float32)
    partial_grad = term.reshape(sources * exp_local * slot_count, model_width)
    shares = lax.psum_scatter(partial_grad, "fsdp", scatter_dimension=0, tiled=True)
    summed = lax.all_to_all(
        shares.reshape(group_count, exp_local, slot_count, model_width),
        "group",
        split_axis=0,
        concat_axis=0,
        tiled=True,
    )
    grad_tokens = (
        jnp.zeros((tokens_in.shape[0], model_width), jnp.float32)
        .at[slot_rows]
        .add(summed.reshape(-1, model_width))
    )
    return (
        grad_tokens.astype(jnp.bfloat16),
        jnp.stack(grads_in_w, axis=0),
        jnp.stack(grads_out_w, axis=0),
    )


def solution(mesh):
    placed = (
        P(("group", "fsdp"), None),
        P(("group", "fsdp"), None),
        P("group", None, "fsdp"),
        P("group", "fsdp", None),
        P(("group", "fsdp"), None, None),
        P(("group", "fsdp"), None),
        P(("group", "fsdp"), None, None),
    )
    return jax.shard_map(
        shards,
        mesh=mesh,
        in_specs=placed,
        out_specs=(P(("group", "fsdp"), None), P("group", None, "fsdp"), P("group", "fsdp", None)),
        check_vma=False,
    )
```

profile of v0, /device:TPU:4, one launch (start us, length us, event | category | flops | bytes accessed | tf_op | source)
XLA Modules:
  0.0 401.1 jit_solution(8017003688771159239)
XLA Ops:
  7.2 0.0 copy-start
  7.2 0.0 all-gather.5.cloned.1.call-start
  7.2 0.9 reshape_squeeze.12
  8.2 4.2 %gather_fusion.1 = bf16[128,2048]{1,0:T(8,128)(2,1)S(1)} fusion(bf16[1024,2048]{1,0:T(8,128)(2,1)} %param.9, s32[1024]{0:T(1024)S(1)} %pad_clamp_fusion), kind=kCustom, calls=%fused_computation.1.clone | custom fusion | bytes 1049088 | tf_op jit(solution)/shard_map/jit(_take)/gather | solution.py:28
  12.4 0.1 broadcast_select_fusion
  12.5 16.3 %all_to_all.15 = bf16[8,1,16,2048]{3,2,1,0:T(8,128)(2,1)} all-to-all(bf16[8,1,16,2048]{3,2,1,0:T(8,128)(2,1)S(1)} %bitcast.43), channel_id=1, replica_groups=mesh['group'=8,'fsdp'=16] {'group'}, dimensions={0} | all-to-all | bytes 1048576 | tf_op jit(solution)/shard_map/all_to_all | solution.py:35
  28.7 0.0 all-gather.5.cloned.1.call-update
  28.8 0.0 all-gather.3.cloned.1.call-start
  28.8 0.1 squeeze.9
  28.9 0.1 iota_compare_fusion
  29.0 0.1 lt.41
  29.1 4.2 %gather_fusion = bf16[128,2048]{1,0:T(8,128)(2,1)S(1)} fusion(bf16[1024,2048]{1,0:T(8,128)(2,1)} %param.10, s32[1024]{0:T(1024)S(1)} %pad_clamp_fusion), kind=kCustom, calls=%fused_computation.clone | custom fusion | bytes 1049088 | tf_op jit(solution)/shard_map/jit(_take)/gather | solution.py:30
  33.3 0.3 multiply_convert_fusion.2
  33.6 15.7 %all_to_all.16 = bf16[8,1,16,2048]{3,2,1,0:T(8,128)(2,1)} all-to-all(bf16[8,1,16,2048]{3,2,1,0:T(8,128)(2,1)S(1)} %bitcast.42), channel_id=1, replica_groups=mesh['group'=8,'fsdp'=16] {'group'}, dimensions={0} | all-to-all | bytes 1048576 | tf_op jit(solution)/shard_map/all_to_all | solution.py:36
  49.2 0.0 all-gather.3.cloned.1.call-update
  49.3 0.0 reduce-scatter.2.cloned.1.call-start
  49.3 36.4 %all-gather.5.cloned.1.call-done = bf16[128,1,16,2048]{3,2,1,0:T(8,128)(2,1)} async-done(((bf16[8,1,16,2048]{3,2,1,0:T(8,128)(2,1)}), bf16[128,1,16,2048]{3,2,1,0:T(8,128)(2,1)}) %all-gather.5.cloned.1.call-update) | async-done | bytes 8388624 | tf_op jit(solution)/shard_map/all_gather | solution.py:39
  85.7 9.4 %fusion.10 = f32[2048,512]{1,0:T(8,128)} fusion(bf16[2048,2048]{1,0:T(8,128)(2,1)} %bitcast.46, bf16[1,2048,512]{2,1,0:T(8,128)(2,1)S(1)} %copy-done), kind=kOutput, calls=%fused_computation.19 | convolution fusion | flops 4294967296 | bytes 14680064 | tf_op jit(solution)/shard_map/dot_general | solution.py:45
  95.1 46.4 %all-gather.3.cloned.1.call-done = bf16[128,1,16,2048]{3,2,1,0:T(8,128)(2,1)} async-done(((bf16[8,1,16,2048]{3,2,1,0:T(8,128)(2,1)}), bf16[128,1,16,2048]{3,2,1,0:T(8,128)(2,1)}) %all-gather.3.cloned.1.call-update) | async-done | bytes 8388624 | tf_op jit(solution)/shard_map/all_gather | solution.py:40
  141.5 12.1 %fusion.6 = bf16[2048,512]{1,0:T(8,128)(2,1)S(1)} fusion(f32[2048,512]{1,0:T(8,128)} %fusion.10, bf16[2048,2048]{1,0:T(8,128)(2,1)} %bitcast.48, bf16[1,512,2048]{2,1,0:T(8,128)(2,1)} %param.12), kind=kOutput, calls=%fused_computation.12 | convolution fusion | flops 4314890240 | bytes 16777216 | tf_op jit(solution)/shard_map/dot_general | solution.py:48
  153.6 6.3 %convolution_bitcast_fusion = f32[128,1,16,2048]{3,0,2,1:T(8,128)S(1)} fusion(bf16[1,2048,512]{2,1,0:T(8,128)(2,1)S(1)} %copy-done, bf16[128,16,512]{2,1,0:T(8,128)(2,1)S(1)} %bitcast.51), kind=kOutput, calls=%fused_computation.3 | convolution fusion | flops 4294967296 | bytes 20971520 | tf_op jit(solution)/shard_map/secf,edf->secd/dot_general | solution.py:64
  159.9 19.4 %copy.16 = f32[128,1,16,2048]{3,2,0,1:T(8,128)} copy(f32[128,1,16,2048]{3,0,2,1:T(8,128)S(1)} %convolution_bitcast_fusion) | data formatting | bytes 33554432 | tf_op jit(solution)/shard_map/secf,edf->secd/transpose | solution.py:64
  179.3 0.0 reduce-scatter.2.cloned.1.call-update
  179.4 0.7 copy-done.2
  180.0 0.1 reshape_squeeze.11
  180.1 10.5 %convolution_bitcast_fusion.2 = f32[1,2048,512]{2,1,0:T(8,128)} fusion(bf16[2048,2048]{1,0:T(8,128)(2,1)} %bitcast.47, bf16[2048,512]{1,0:T(8,128)(2,1)} %copy-done.5), kind=kOutput, calls=%fused_computation.17 | convolution fusion | flops 4294967296 | bytes 14680064 | tf_op jit(solution)/shard_map/dot_general | solution.py:53
  190.7 172.3 %reduce-scatter.2.cloned.1.call-done = f32[128,2048]{1,0:T(8,128)} async-done(((f32[2048,2048]{1,0:T(8,128)}), f32[128,2048]{1,0:T(8,128)}) %reduce-scatter.2.cloned.1.call-update) | async-done | bytes 1048592 | tf_op jit(solution)/shard_map/reduce_scatter | solution.py:66
  363.0 6.9 %all-to-all-start.2 = ((f32[8,1,16,2048]{3,2,1,0:T(8,128)}), f32[8,1,16,2048]{3,2,1,0:T(8,128)S(1)}, u32[]{:S(2)}, u32[]{:S(2)}) async-start(f32[8,1,16,2048]{3,2,1,0:T(8,128)} %bitcast.44), calls=%async_computation.3 | async-start | bytes 2097152 | tf_op jit(solution)/shard_map/all_to_all | solution.py:67
  369.9 11.5 %convolution_bitcast_fusion.1 = f32[1,512,2048]{2,1,0:T(8,128)} fusion(bf16[2048,2048]{1,0:T(8,128)(2,1)} %bitcast.49, f32[2048,512]{1,0:T(8,128)} %fusion.10), kind=kOutput, calls=%fused_computation.16 | convolution fusion | flops 4304404480 | bytes 16777216 | tf_op jit(solution)/shard_map/dot_general | solution.py:58
  381.4 1.3 all-to-all-done.2
  382.7 5.8 %scatter_custom_fusion = f32[1024,2048]{1,0:T(8,128)} fusion(s32[128]{0:T(128)S(1)} %fusion.18, f32[128,2048]{1,0:T(8,128)S(1)} %bitcast.45, f32[]{:T(128)} %constant.0.clone.1), kind=kCustom, calls=%fused_computation.14 | custom fusion | flops 262144 | bytes 8388612 | tf_op jit(solution)/shard_map/scatter-add | solution.py:77
  388.5 6.0 %convert_element_type.18 = bf16[1024,2048]{1,0:T(8,128)(2,1)} convert(f32[1024,2048]{1,0:T(8,128)} %scatter_custom_fusion) | non-fusion elementwise | flops 2097152 | bytes 12582912 | tf_op jit(solution)/shard_map/convert_element_type | solution.py:80
  (15 shorter events, 0.1 us)
Async XLA Ops:
  7.2 78.5 %copy-start = (bf16[1,2048,512]{2,1,0:T(8,128)(2,1)S(1)}, bf16[1,2048,512]{2,1,0:T(8,128)(2,1)}, u32[]{:S(2)}) copy-start(bf16[1,2048,512]{2,1,0:T(8,128)(2,1)} %param.11) | copy-start | bytes 6291460
  7.2 21.6 %copy-start.3 = (f32[1,8,16]{2,1,0:T(8,128)S(1)}, f32[1,8,16]{2,1,0:T(8,128)}, u32[]{:S(2)}) copy-start(f32[1,8,16]{2,1,0:T(8,128)} %param.15) | copy-start | bytes 1540
  7.2 21.7 %copy-start.4 = (s32[1,8]{1,0:T(1,128)S(1)}, s32[1,8]{1,0:T(1,128)}, u32[]{:S(2)}) copy-start(s32[1,8]{1,0:T(1,128)} %param.14) | copy-start | bytes 100
  7.2 78.5 %all-gather.5.cloned.1.call-start = ((), (), s32[]{:S(2)}) async-start(), calls=%async_computation.5 | async-start | bytes 8912896 | tf_op jit(solution)/shard_map/all_gather | solution.py:39
  28.8 112.7 %all-gather.3.cloned.1.call-start = ((), (), s32[]{:S(2)}) async-start(), calls=%async_computation.4 | async-start | bytes 8912896 | tf_op jit(solution)/shard_map/all_gather | solution.py:40
  49.3 313.7 %reduce-scatter.2.cloned.1.call-start = ((), (), s32[]{:S(2)}) async-start(), calls=%async_computation.6 | async-start | bytes 17825792 | tf_op jit(solution)/shard_map/reduce_scatter | solution.py:66
  153.6 6.3 %copy-start.5 = (bf16[2048,512]{1,0:T(8,128)(2,1)}, bf16[2048,512]{1,0:T(8,128)(2,1)S(1)}, u32[]{:S(2)}) copy-start(bf16[2048,512]{1,0:T(8,128)(2,1)S(1)} %fusion.6) | copy-start | bytes 6291460
  179.3 0.7 copy-start.2
  363.0 19.7 %all-to-all-start.2 = ((f32[8,1,16,2048]{3,2,1,0:T(8,128)}), f32[8,1,16,2048]{3,2,1,0:T(8,128)S(1)}, u32[]{:S(2)}, u32[]{:S(2)}) async-start(f32[8,1,16,2048]{3,2,1,0:T(8,128)} %bitcast.44), calls=%async_computation.3 | async-start | bytes 2097152 | tf_op jit(solution)/shard_map/all_to_all | solution.py:67
  382.7 11.9 %copy-start.1 = (bf16[1,2048,512]{2,1,0:T(8,128)(2,1)S(1)}, bf16[1,2048,512]{2,1,0:T(8,128)(2,1)}, u32[]{:S(2)}) copy-start(bf16[1,2048,512]{2,1,0:T(8,128)(2,1)} %param.11) | copy-start | bytes 6291460
Sparse Core Ops, SparseCore 0:
  28.9 56.7 all-gather.4
  87.4 54.0 all-gather.2
  179.5 183.4 reduce-scatter.1
where the time goes:
time: 404 us; the launch traced here: 401 us
  waiting for transfers between devices  256 us (63%)
  matrix products  49.9 us (12%)
  blocking collectives  31.9 us (8%)
  local copies, waits for them, and re-layouts  29.6 us (7%)
  between operations  13.9 us (3%)
  other arithmetic  12.4 us (3%)
  starting transfers between devices  7.07 us (2%)
    reduce_scatter x1, waiting for transfers between devices, shards(): lax.psum_scatter(partial_grad, 'fsdp', scatter_dimension=0, tiled=True)  172 us
    all_gather x1, waiting for transfers between devices, shards(): lax.all_gather(near_grad, 'fsdp', axis=0, tiled=True)  46.4 us
    all_gather x1, waiting for transfers between devices, shards(): lax.all_gather(near_x, 'fsdp', axis=0, tiled=True)  36.4 us
    transpose x1, local copies, waits for them, and re-layouts, shards(): jnp.einsum('secf,edf->secd', stacked_grad, w_in, preferred_element_type=j...  19.4 us
    all_to_all x1, blocking collectives, shards(): lax.all_to_all(picked_x, 'group', split_axis=0, concat_axis=0, tiled=True)  16.3 us
    all_to_all x1, blocking collectives, shards(): lax.all_to_all(picked_grad, 'group', split_axis=0, concat_axis=0, tiled=T...  15.7 us
    dot_general x1, matrix products, shards(): lax.dot_general(expert_grad, w_out[0], (((1,), (1,)), ((), ())), preferre...  12.1 us
    dot_general x1, matrix products, shards(): lax.dot_general(activation, expert_grad, (((0,), (0,)), ((), ())), prefer...  11.5 us
  transfers between devices with their start and end apart: 4, of which 4 were waited for; matrix products, arithmetic and copies ran while one was open for 9% of the time, Pallas kernels for 0%

commit v1 on v0

v1 whole, which is shorter than its diff:
```python
import functools

import jax
import jax.numpy as jnp
from jax import lax
from jax.experimental import pallas as pl
from jax.experimental.pallas import tpu as pltpu
from jax.sharding import PartitionSpec as P

MESH = pl.DeviceIdType.MESH
gelu_coef = 0.7978845608028654
BF = jnp.bfloat16
F32 = jnp.float32


def gelu_parts(hidden):
    inner_arg = gelu_coef * (hidden + 0.044715 * hidden * hidden * hidden)
    tangent = jnp.tanh(inner_arg)
    activation = 0.5 * hidden * (1.0 + tangent)
    slope = 0.5 * (1.0 + tangent) + 0.5 * hidden * (1.0 - tangent * tangent) * gelu_coef * (
        1.0 + 3.0 * 0.044715 * hidden * hidden
    )
    return (activation, slope)


def slot_column(table):
    experts, slots = table.shape
    spread = jnp.concatenate(
        [jnp.broadcast_to(table[e : e + 1, :], (slots, slots)) for e in range(experts)], axis=0
    )
    row = lax.broadcasted_iota(jnp.int32, spread.shape, 0)
    lane = lax.broadcasted_iota(jnp.int32, spread.shape, 1)
    picked = jnp.where(lax.rem(row, slots) == lane, spread, jnp.zeros_like(spread))
    return jnp.sum(picked, axis=1, keepdims=True)


def one_hot_rows(chosen, length):
    column = slot_column(chosen.astype(F32)).astype(jnp.int32)
    lanes = lax.broadcasted_iota(jnp.int32, (column.shape[0], length), 1)
    return jnp.where(lanes == column, jnp.float32(1.0), jnp.float32(0.0)).astype(BF)


def pick_kernel(chosen_ref, counts_ref, gates_ref, x_ref, g_ref, px_ref, pg_ref):
    chosen = chosen_ref[0]
    slot_iota = lax.broadcasted_iota(jnp.int32, chosen.shape, 1)
    experts = chosen.shape[0]
    lane = lax.broadcasted_iota(jnp.int32, (experts, experts), 1)
    row = lax.broadcasted_iota(jnp.int32, (experts, experts), 0)
    limit = jnp.sum(
        jnp.where(lane == row, jnp.broadcast_to(counts_ref[...].astype(F32), (experts, experts)), 0.0),
        axis=1,
        keepdims=True,
    )
    live = jnp.where(slot_iota.astype(F32) < limit, gates_ref[0], jnp.float32(0.0))
    gate = slot_column(live)
    hot = one_hot_rows(chosen, x_ref.shape[0])
    px_ref[...] = jnp.dot(hot, x_ref[...], preferred_element_type=F32).astype(BF)
    pg_ref[...] = (gate * jnp.dot(hot, g_ref[...], preferred_element_type=F32)).astype(BF)


def pick_rows(tokens_in, out_grad, chosen, counts, gates):
    length, width = tokens_in.shape
    rows = chosen.shape[1] * chosen.shape[2]
    tile = 512
    whole = lambda a: pl.BlockSpec(a.shape, lambda i: (0,) * a.ndim)
    return pl.pallas_call(
        pick_kernel,
        grid=(width // tile,),
        in_specs=[
            whole(chosen),
            whole(counts),
            whole(gates),
            pl.BlockSpec((length, tile), lambda i: (0, i)),
            pl.BlockSpec((length, tile), lambda i: (0, i)),
        ],
        out_specs=[pl.BlockSpec((rows, tile), lambda i: (0, i))] * 2,
        out_shape=[jax.ShapeDtypeStruct((rows, width), BF)] * 2,
        name="pick_rows",
    )(chosen, counts, gates, tokens_in, out_grad)


def spread_kernel(chosen_ref, ret_ref, out_ref):
    hot = one_hot_rows(chosen_ref[0], out_ref.shape[0])
    out_ref[...] = lax.dot_general(
        hot, ret_ref[...], (((0,), (0,)), ((), ())), preferred_element_type=F32
    ).astype(BF)


def spread_rows(chosen, ret, length):
    rows, width = ret.shape
    tile = 512
    return pl.pallas_call(
        spread_kernel,
        grid=(width // tile,),
        in_specs=[
            pl.BlockSpec(chosen.shape, lambda i: (0, 0, 0)),
            pl.BlockSpec((rows, tile), lambda i: (0, i)),
        ],
        out_specs=pl.BlockSpec((length, tile), lambda i: (0, i)),
        out_shape=jax.ShapeDtypeStruct((length, width), BF),
        name="spread_rows",
    )(chosen, ret)


OWN, YY, ZM, ZP, OO, OY, MY, PY = range(8)
PIECE_M, PIECE_P, PIECE_Y, PIECE_A, PIECE_B, PIECE_OY, PIECE_MY, PIECE_PY = range(8)
RS_Y1, RS_A, RS_B, RS_LM, RS_LP, RS_M, RS_P, RS_Y = range(8)


def layer_kernel(
    groups,
    px,
    pg,
    win_hbm,
    wout_hbm,
    ret_ref,
    dwin_hbm,
    dwout_hbm,
    xbuf,
    gbuf,
    win,
    wout,
    act_t,
    hg_t,
    slope_buf,
    sg,
    pair,
    rs_y1,
    rs_half,
    rs_leaf,
    rs_last,
    fin,
    back,
    tiles,
    a_send,
    a_recv,
    own_sem,
    w_sem,
    ag_send,
    ag_recv,
    core_send,
    core_recv,
    pr_send,
    pr_recv,
    rs_send,
    rs_recv,
    d_send,
    d_recv,
    t_sem,
):
    g = lax.axis_index("group")
    f = lax.axis_index("fsdp")
    z, l, c = f // 4, lax.rem(f // 2, 2), lax.rem(f, 2)
    up, down, far = lax.rem(z + 1, 4), lax.rem(z + 3, 4), lax.rem(z + 2, 4)
    unit_of = {
        OWN: z * 2 + l,
        YY: z * 2 + (1 - l),
        ZM: down * 2 + l,
        ZP: up * 2 + l,
        OO: far * 2 + l,
        OY: far * 2 + (1 - l),
        MY: down * 2 + (1 - l),
        PY: up * 2 + (1 - l),
    }
    to_up, to_down = up * 4 + l * 2 + c, down * 4 + l * 2 + c
    to_y = z * 4 + (1 - l) * 2 + c
    to_core = z * 4 + l * 2 + (1 - c)
    CH = 128
    HALF = CH // 2
    SL = CH // groups

    def mine(u, start=0, size=CH):
        return pl.ds(pl.multiple_of((unit_of[u] * 2 + c) * CH + start, 16), size)

    def other(u):
        return pl.ds(pl.multiple_of((unit_of[u] * 2 + (1 - c)) * CH, 16), CH)

    barrier = pltpu.get_barrier_semaphore()
    for k in range(1, groups):
        pl.semaphore_signal(barrier, inc=1, device_id=(lax.rem(g + k, groups), f), device_id_type=MESH)
    for d in (to_up, to_down, to_y, to_core):
        pl.semaphore_signal(barrier, inc=1, device_id=(g, d), device_id_type=MESH)
    w_copies = [
        pltpu.make_async_copy(win_hbm.at[0], win, w_sem.at[0]),
        pltpu.make_async_copy(wout_hbm.at[0], wout, w_sem.at[1]),
    ]
    for w in w_copies:
        w.start()
    pl.semaphore_wait(barrier, groups - 1 + 4)

    bufs = (xbuf, gbuf)
    picked = (px, pg)
    pending = []

    def a_copy(a, k):
        dest = lax.rem(g + k, groups)
        return pltpu.make_async_remote_copy(
            src_ref=picked[a].at[pl.ds(pl.multiple_of(dest * SL, 16), SL)],
            dst_ref=bufs[a].at[pl.ds(pl.multiple_of(f * CH + g * SL, 16), SL)],
            send_sem=a_send.at[a, k - 1],
            recv_sem=a_recv.at[a, k - 1],
            device_id=(dest, f),
            device_id_type=MESH,
        )

    def a_arrival(a, k):
        source = lax.rem(g + groups - k, groups)
        here = bufs[a].at[pl.ds(pl.multiple_of(f * CH + source * SL, 16), SL)]
        return pltpu.make_async_remote_copy(
            src_ref=here,
            dst_ref=here,
            send_sem=a_send.at[a, k - 1],
            recv_sem=a_recv.at[a, k - 1],
            device_id=(source, f),
            device_id_type=MESH,
        )

    own_copies = []
    for a in range(2):
        for k in range(1, groups):
            copy = a_copy(a, k)
            copy.start()
            pending.append(copy)
        own = pltpu.make_async_copy(
            picked[a].at[pl.ds(pl.multiple_of(g * SL, 16), SL)],
            bufs[a].at[pl.ds(pl.multiple_of(f * CH + g * SL, 16), SL)],
            own_sem.at[a],
        )
        own.start()
        own_copies.append(own)

    def ag(a, rows, dest, piece, send):
        copy = pltpu.make_async_remote_copy(
            src_ref=bufs[a].at[rows],
            dst_ref=bufs[a].at[rows],
            send_sem=ag_send.at[a, send],
            recv_sem=ag_recv.at[a, piece],
            device_id=(g, dest),
            device_id_type=MESH,
        )
        return copy

    def ag_start(a, rows, dest, piece):
        copy = ag(a, rows, dest, piece, piece)
        copy.start()
        pending.append(copy)

    def ag_wait(a, rows, piece):
        ag(a, rows, to_y, piece, piece).wait_recv()

    def core(a, rows, u):
        return pltpu.make_async_remote_copy(
            src_ref=bufs[a].at[rows],
            dst_ref=bufs[a].at[rows],
            send_sem=core_send.at[a, u],
            recv_sem=core_recv.at[a, u],
            device_id=(g, to_core),
            device_id_type=MESH,
        )

    def core_start(a, u):
        copy = core(a, mine(u), u)
        copy.start()
        pending.append(copy)

    def core_wait(a, u):
        core(a, other(u), u).wait_recv()

    def unit_rows(u):
        return pl.ds(pl.multiple_of(unit_of[u] * 2 * CH, 2 * CH), 2 * CH)

    def forward(u):
        core_wait(0, u)
        rows = unit_rows(u)
        hidden = jnp.dot(xbuf[rows, :], win[...], preferred_element_type=F32)
        activation, slope = gelu_parts(hidden)
        act_t[:, rows] = activation.T.astype(BF)
        slope_buf[rows, :] = slope

    def pair_copy(u, rows):
        return pltpu.make_async_remote_copy(
            src_ref=sg.at[rows],
            dst_ref=pair.at[unit_of[u]],
            send_sem=pr_send.at[u],
            recv_sem=pr_recv.at[u],
            device_id=(g, to_core),
            device_id_type=MESH,
        )

    def backward(u):
        core_wait(1, u)
        rows = unit_rows(u)
        back_hidden = lax.dot_general(
            gbuf[rows, :], wout[...], (((1,), (1,)), ((), ())), preferred_element_type=F32
        )
        hidden_grad = back_hidden * slope_buf[rows, :]
        hg_t[:, rows] = hidden_grad.T.astype(BF)
        hidden_grad = hidden_grad.astype(BF)

        @pl.loop(0, 4)
        def _(j):
            cols = pl.ds(pl.multiple_of(j * 512, 512), 512)
            part = lax.dot_general(
                hidden_grad, win[cols, :], (((1,), (1,)), ((), ())), preferred_element_type=F32
            )
            sg[rows, cols] = part.astype(BF)

        copy = pair_copy(u, other(u))
        copy.start()
        pending.append(copy)

    def accumulate(base, size, load):
        @pl.loop(0, size // 16)
        def _(i):
            rows = pl.ds(pl.multiple_of(base + i * 16, 16), 16)
            total = sg[rows, :].astype(F32)
            sg[rows, :] = (total + load(i)).astype(BF)

    def chunk_start(u):
        return (unit_of[u] * 2 + c) * CH

    def block(i):
        return pl.ds(pl.multiple_of(i * 16, 16), 16)

    def pair_add(u):
        pair_copy(u, mine(u)).wait_recv()
        slab = pair.at[unit_of[u]]
        accumulate(chunk_start(u), CH, lambda i: slab[block(i), :].astype(F32))

    def rs(rows, dst, idx, dest):
        return pltpu.make_async_remote_copy(
            src_ref=sg.at[rows],
            dst_ref=dst,
            send_sem=rs_send.at[idx],
            recv_sem=rs_recv.at[idx],
            device_id=(g, dest),
            device_id_type=MESH,
        )

    def rs_start(rows, dst, idx, dest):
        copy = rs(rows, dst, idx, dest)
        copy.start()
        pending.append(copy)

    def rs_wait(dst, idx, size=CH):
        rs(mine(OWN, 0, size), dst, idx, to_y).wait_recv()

    def tile_copies(slot, j):
        cols = pl.ds(pl.multiple_of(j * 256, 256), 256)
        return (
            pltpu.make_async_copy(tiles[0].at[slot], dwin_hbm.at[0, cols, :], t_sem.at[0, slot]),
            pltpu.make_async_copy(tiles[1].at[slot], dwout_hbm.at[0, :, cols], t_sem.at[1, slot]),
        )

    def weight_tiles(first, last):
        @pl.loop(first, last)
        def _(j):
            slot = lax.rem(j, 2)
            cols = pl.ds(pl.multiple_of(j * 256, 256), 256)
            into, outof = tile_copies(slot, j)

            @pl.when(j >= 2)
            def _():
                into.wait()
                outof.wait()

            tiles[0][slot] = jnp.dot(hg_t[...], xbuf[:, cols], preferred_element_type=F32).T
            into.start()
            tiles[1][slot] = jnp.dot(act_t[...], gbuf[:, cols], preferred_element_type=F32)
            outof.start()

    for a in range(2):
        own_copies[a].wait()
        for k in range(1, groups):
            a_arrival(a, k).wait_recv()
        ag_start(a, mine(OWN), to_up, PIECE_M)
        ag_start(a, mine(OWN), to_down, PIECE_P)
        ag_start(a, mine(OWN), to_y, PIECE_Y)
        core_start(a, OWN)
    for w in w_copies:
        w.wait()
    forward(OWN)
    backward(OWN)

    ag_wait(0, mine(ZM), PIECE_M)
    ag_start(0, mine(ZM, 0, HALF), to_up, PIECE_A)
    core_start(0, ZM)
    ag_wait(0, mine(ZP), PIECE_P)
    ag_start(0, mine(ZP, HALF, HALF), to_down, PIECE_B)
    core_start(0, ZP)
    ag_wait(0, mine(YY), PIECE_Y)
    core_start(0, YY)
    pair_add(OWN)
    forward(ZM)
    forward(ZP)
    forward(YY)
    ag_wait(1, mine(ZM), PIECE_M)
    ag_start(1, mine(ZM, 0, HALF), to_up, PIECE_A)
    core_start(1, ZM)
    ag_wait(1, mine(ZP), PIECE_P)
    ag_start(1, mine(ZP, HALF, HALF), to_down, PIECE_B)
    core_start(1, ZP)
    ag_start(0, mine(YY), to_up, PIECE_MY)
    ag_start(0, mine(YY), to_down, PIECE_PY)
    ag_wait(1, mine(YY), PIECE_Y)
    ag_start(1, mine(YY), to_up, PIECE_MY)
    ag_start(1, mine(YY), to_down, PIECE_PY)
    core_start(1, YY)
    backward(ZM)
    backward(ZP)
    pair_add(ZM)

    ag_wait(0, mine(OO, 0, HALF), PIECE_A)
    ag_wait(0, mine(OO, HALF, HALF), PIECE_B)
    ag_start(0, mine(OO), to_y, PIECE_OY)
    core_start(0, OO)
    backward(YY)
    pair_add(ZP)
    ag_wait(1, mine(OO, 0, HALF), PIECE_A)
    ag_wait(1, mine(OO, HALF, HALF), PIECE_B)
    ag_start(1, mine(OO), to_y, PIECE_OY)
    core_start(1, OO)
    forward(OO)
    pair_add(YY)
    backward(OO)

    ag_wait(0, mine(OY), PIECE_OY)
    core_start(0, OY)
    pair_add(OO)
    forward(OY)
    ag_wait(0, mine(MY), PIECE_MY)
    core_start(0, MY)
    ag_wait(0, mine(PY), PIECE_PY)
    core_start(0, PY)
    forward(MY)
    forward(PY)
    ag_wait(1, mine(OY), PIECE_OY)
    core_start(1, OY)
    backward(OY)
    ag_wait(1, mine(MY), PIECE_MY)
    core_start(1, MY)
    ag_wait(1, mine(PY), PIECE_PY)
    core_start(1, PY)
    pair_add(OY)
    rs_start(mine(OY), rs_y1, RS_Y1, to_y)
    backward(MY)
    backward(PY)

    pair_add(MY)
    rs_start(mine(MY), rs_leaf.at[1], RS_LP, to_down)
    pair_add(PY)
    rs_wait(rs_y1, RS_Y1)
    accumulate(chunk_start(OO), CH, lambda i: rs_y1[block(i), :].astype(F32))
    rs_start(mine(OO, 0, HALF), rs_half.at[0], RS_A, to_down)
    rs_start(mine(OO, HALF, HALF), rs_half.at[1], RS_B, to_up)
    rs_start(mine(PY), rs_leaf.at[0], RS_LM, to_up)
    weight_tiles(0, 2)
    rs_wait(rs_half.at[0], RS_A, HALF)
    accumulate(chunk_start(ZM), HALF, lambda i: rs_half[0, block(i), :].astype(F32))
    rs_start(mine(ZM), rs_last.at[1], RS_P, to_down)
    rs_wait(rs_half.at[1], RS_B, HALF)
    accumulate(chunk_start(ZP) + HALF, HALF, lambda i: rs_half[1, block(i), :].astype(F32))
    rs_start(mine(ZP), rs_last.at[0], RS_M, to_up)
    weight_tiles(2, 6)
    rs_wait(rs_leaf.at[0], RS_LM)
    rs_wait(rs_leaf.at[1], RS_LP)
    accumulate(
        chunk_start(YY),
        CH,
        lambda i: rs_leaf[0, block(i), :].astype(F32) + rs_leaf[1, block(i), :].astype(F32),
    )
    rs_start(mine(YY), rs_last.at[2], RS_Y, to_y)
    weight_tiles(6, 8)
    rs_wait(rs_last.at[0], RS_M)
    rs_wait(rs_last.at[1], RS_P)
    rs_wait(rs_last.at[2], RS_Y)

    @pl.loop(0, CH // 16)
    def _(i):
        rows = pl.ds(pl.multiple_of(chunk_start(OWN) + i * 16, 16), 16)
        total = sg[rows, :].astype(F32) + rs_last[0, block(i), :].astype(F32)
        total = total + rs_last[1, block(i), :].astype(F32) + rs_last[2, block(i), :].astype(F32)
        fin[block(i), :] = total.astype(BF)

    def d_copy(k):
        dest = lax.rem(g + k, groups)
        return pltpu.make_async_remote_copy(
            src_ref=fin.at[pl.ds(pl.multiple_of(dest * SL, 16), SL)],
            dst_ref=back.at[pl.ds(pl.multiple_of(g * SL, 16), SL)],
            send_sem=d_send.at[k - 1],
            recv_sem=d_recv.at[k - 1],
            device_id=(dest, f),
            device_id_type=MESH,
        )

    def d_arrival(k):
        source = lax.rem(g + groups - k, groups)
        return pltpu.make_async_remote_copy(
            src_ref=fin.at[pl.ds(0, SL)],
            dst_ref=back.at[pl.ds(pl.multiple_of(source * SL, 16), SL)],
            send_sem=d_send.at[k - 1],
            recv_sem=d_recv.at[k - 1],
            device_id=(source, f),
            device_id_type=MESH,
        )

    for k in range(1, groups):
        copy = d_copy(k)
        copy.start()
        pending.append(copy)
    own_rows = pl.ds(pl.multiple_of(g * SL, 16), SL)
    back[own_rows, :] = fin[own_rows, :]
    for slot in range(2):
        into, outof = tile_copies(slot, 6 + slot)
        into.wait()
        outof.wait()
    for k in range(1, groups):
        d_arrival(k).wait_recv()
    ret_ref[...] = back[...]
    for copy in pending:
        copy.wait_send()


def layer(px, pg, w_in, w_out):
    groups = lax.axis_size("group")
    rows, width = px.shape
    hidden = w_in.shape[2]
    total = rows * lax.axis_size("fsdp")
    vmem, dma = pltpu.VMEM, pltpu.SemaphoreType.DMA
    return pl.pallas_call(
        functools.partial(layer_kernel, groups),
        out_shape=[
            jax.ShapeDtypeStruct((rows, width), BF),
            jax.ShapeDtypeStruct((1, width, hidden), F32),
            jax.ShapeDtypeStruct((1, hidden, width), F32),
        ],
        in_specs=[pl.BlockSpec(memory_space=pltpu.VMEM)] * 2 + [pl.BlockSpec(memory_space=pl.ANY)] * 2,
        out_specs=[pl.BlockSpec(memory_space=pltpu.VMEM)] + [pl.BlockSpec(memory_space=pl.ANY)] * 2,
        scratch_shapes=[
            vmem((total, width), BF),
            vmem((total, width), BF),
            vmem((width, hidden), BF),
            vmem((hidden, width), BF),
            vmem((hidden, total), BF),
            vmem((hidden, total), BF),
            vmem((total, hidden), F32),
            vmem((total, width), BF),
            vmem((8, rows, width), BF),
            vmem((rows, width), BF),
            vmem((2, rows // 2, width), BF),
            vmem((2, rows, width), BF),
            vmem((3, rows, width), BF),
            vmem((rows, width), BF),
            vmem((rows, width), BF),
            [vmem((2, 256, hidden), F32), vmem((2, hidden, 256), F32)],
            dma((2, groups - 1)),
            dma((2, groups - 1)),
            dma((2,)),
            dma((2,)),
            dma((2, 8)),
            dma((2, 8)),
            dma((2, 8)),
            dma((2, 8)),
            dma((8,)),
            dma((8,)),
            dma((8,)),
            dma((8,)),
            dma((groups - 1,)),
            dma((groups - 1,)),
            dma((2, 2)),
        ],
        compiler_params=pltpu.CompilerParams(
            collective_id=0, has_side_effects=True, vmem_limit_bytes=62 * 1024 * 1024
        ),
        name="layer",
    )(px, pg, w_in, w_out)


def shards(tokens_in, out_grad, w_in, w_out, chosen, counts, gates):
    px, pg = pick_rows(tokens_in, out_grad, chosen, counts, gates)
    ret, grad_w_in, grad_w_out = layer(px, pg, w_in, w_out)
    grad_in = spread_rows(chosen, ret, tokens_in.shape[0])
    return (grad_in, grad_w_in, grad_w_out)


def solution(mesh):
    placed = (
        P(("group", "fsdp"), None),
        P(("group", "fsdp"), None),
        P("group", None, "fsdp"),
        P("group", "fsdp", None),
        P(("group", "fsdp"), None, None),
        P(("group", "fsdp"), None),
        P(("group", "fsdp"), None, None),
    )
    return jax.shard_map(
        shards,
        mesh=mesh,
        in_specs=placed,
        out_specs=(P(("group", "fsdp"), None), P("group", None, "fsdp"), P("group", "fsdp", None)),
        check_vma=False,
    )
```

time: 404 us -> 158 us (0.39)
  waiting for transfers between devices: 256 us -> 0 us
  Pallas kernels: 0 us -> 150 us
  matrix products: 49.9 us -> 0 us
  blocking collectives: 31.9 us -> 0 us
  local copies, waits for them, and re-layouts: 29.6 us -> 6.83 us
  between operations: 13.9 us -> 0.64 us
  other arithmetic: 12.4 us -> 0 us
  starting transfers between devices: 7.07 us -> 0 us
    reduce_scatter x1 -> x0, waiting for transfers between devices: 172 us -> none  [shards(): lax.psum_scatter(partial_grad, 'fsdp', scatter_dimension=0, tiled=True)]
    pallas_call x0 -> x3, Pallas kernels: none -> 150 us  [the longest x1 140 us: layer(): pl.pallas_call(functools.partial(layer_kernel, groups), out_shape=[jax.Sh...]
    all_gather x2 -> x0, waiting for transfers between devices: 82.7 us -> none  [the longest x1 46.4 us: shards(): lax.all_gather(near_grad, 'fsdp', axis=0, tiled=True)]
    dot_general x5 -> x0, matrix products: 49.9 us -> none  [the longest x1 12.1 us: shards(): lax.dot_general(expert_grad, w_out[0], (((1,), (1,)), ((), ())), preferre...]
    all_to_all x2 -> x0, blocking collectives: 31.9 us -> none  [the longest x1 16.3 us: shards(): lax.all_to_all(picked_x, 'group', split_axis=0, concat_axis=0, tiled=True)]
    transpose x1 -> x0, local copies, waits for them, and re-layouts: 19.4 us -> none  [shards(): jnp.einsum('secf,edf->secd', stacked_grad, w_in, preferred_element_type=j...]
    gather x2 -> x0, local copies, waits for them, and re-layouts: 8.34 us -> none  [the longest x1 4.17 us: shards(): jnp.take(out_grad, slot_rows, axis=0).astype(jnp.float32)]
    all_to_all x1 -> x0, starting transfers between devices: 6.94 us -> none  [shards(): lax.all_to_all(shares.reshape(group_count, exp_local, slot_count, model_w...]
  transfers between devices with their start and end apart: 4 -> 0, of which waited for: 4 -> 0; matrix products, arithmetic and copies ran while one was open for 9% -> 0% of each run, Pallas kernels for 0% -> 0%
where the time goes in v1:
time: 158 us
  Pallas kernels  150 us (95%)
  local copies, waits for them, and re-layouts  6.83 us (4%)
    pallas_call x1, Pallas kernels, layer(): pl.pallas_call(functools.partial(layer_kernel, groups), out_shape=[jax.Sh...  140 us
    unnamed x4, local copies, waits for them, and re-layouts  6.83 us
    pallas_call x1, Pallas kernels, pick_rows(): pl.pallas_call(pick_kernel, grid=(width // tile,), in_specs=[whole(chosen...  5.73 us
    pallas_call x1, Pallas kernels, spread_rows(): pl.pallas_call(spread_kernel, grid=(width // tile,), in_specs=[pl.BlockSp...  4.85 us

profile of v1, /device:TPU:4, one launch (start us, length us, event | category | flops | bytes accessed | tf_op | source)
XLA Modules:
  0.0 157.9 jit_solution(13518028282505986229)
XLA Ops:
  0.6 5.7 %pick_rows.1 = (bf16[128,2048]{1,0:T(8,128)(2,1)}, bf16[128,2048]{1,0:T(8,128)(2,1)}) custom-call(s32[1,8,16]{2,1,0:T(8,128)} %chosen_ref.3, s32[1,8]{1,0:T(1,128)} %counts_ref.1, f32[1,8,16]{2,1,0:T(8,128)} %gates_ref.1, bf16[1024,2048]{1,0:T(8,128)(2,1)} %x_ref.1, bf16[1024,2048]{1,0:T(8,128)(2,1)} %g_ref.1), custom_call_target="tpu_custom_call" | custom-call | tf_op jit(solution)/shard_map/pick_rows/pallas_call | solution.py:66
  6.4 139.8 %layer.1 = (bf16[128,2048]{1,0:T(8,128)(2,1)}, f32[1,2048,512]{2,1,0:T(8,128)}, f32[1,512,2048]{2,1,0:T(8,128)}) custom-call(bf16[128,2048]{1,0:T(8,128)(2,1)} %get-tuple-element.8.px, bf16[128,2048]{1,0:T(8,128)(2,1)} %get-tuple-element.9.pg, bf16[1,2048,512]{2,1,0:T(8,128)(2,1)} %win_hbm.1, bf16[1,512,2048]{2,1,0:T(8,128)(2,1)} %wout_hbm.1), custom_call_target="tpu_custom_call" | custom-call | tf_op jit(solution)/shard_map/layer/pallas_call | solution.py:530
  146.2 4.9 %spread_rows.1 = bf16[1024,2048]{1,0:T(8,128)(2,1)} custom-call(s32[1,8,16]{2,1,0:T(8,128)} %chosen_ref.3, bf16[128,2048]{1,0:T(8,128)(2,1)} %get-tuple-element.10.ret_ref), custom_call_target="tpu_custom_call" | custom-call | tf_op jit(solution)/shard_map/spread_rows/pallas_call | solution.py:92
  151.1 0.0 copy-start
  151.1 4.8 %copy.12 = f32[1,2048,512]{2,1,0:T(8,128)} copy(f32[1,2048,512]{2,1,0:T(8,128)} %get-tuple-element.17) | data formatting | bytes 8388608
  155.9 0.0 copy-done
  155.9 2.0 %copy.13 = f32[1,512,2048]{2,1,0:T(8,128)} copy(f32[1,512,2048]{2,1,0:T(8,128)S(1)} %copy-done) | data formatting | bytes 8388608
Async XLA Ops:
  151.1 4.8 %copy-start = (f32[1,512,2048]{2,1,0:T(8,128)S(1)}, f32[1,512,2048]{2,1,0:T(8,128)}, u32[]{:S(2)}) copy-start(f32[1,512,2048]{2,1,0:T(8,128)} %get-tuple-element.18) | copy-start | bytes 12582916

commit v2 on v0

v2 whole, which is shorter than its diff:
```python
import jax
import jax.numpy as jnp
from jax import lax
from jax.experimental import pallas as pl
from jax.experimental.pallas import tpu as pltpu
from jax.sharding import PartitionSpec as P

MESH = pl.DeviceIdType.MESH
gelu_coef = 0.7978845608028654
BF = jnp.bfloat16
F32 = jnp.float32


def gelu_parts(hidden):
    inner_arg = gelu_coef * (hidden + 0.044715 * hidden * hidden * hidden)
    tangent = jnp.tanh(inner_arg)
    activation = 0.5 * hidden * (1.0 + tangent)
    slope = 0.5 * (1.0 + tangent) + 0.5 * hidden * (1.0 - tangent * tangent) * gelu_coef * (
        1.0 + 3.0 * 0.044715 * hidden * hidden
    )
    return (activation, slope)


def slot_column(table):
    experts, slots = table.shape
    spread = jnp.concatenate(
        [jnp.broadcast_to(table[e : e + 1, :], (slots, slots)) for e in range(experts)], axis=0
    )
    row = lax.broadcasted_iota(jnp.int32, spread.shape, 0)
    lane = lax.broadcasted_iota(jnp.int32, spread.shape, 1)
    picked = jnp.where(lax.rem(row, slots) == lane, spread, jnp.zeros_like(spread))
    return jnp.sum(picked, axis=1, keepdims=True)


def one_hot_rows(chosen, length):
    column = slot_column(chosen.astype(F32)).astype(jnp.int32)
    lanes = lax.broadcasted_iota(jnp.int32, (column.shape[0], length), 1)
    return jnp.where(lanes == column, jnp.float32(1.0), jnp.float32(0.0)).astype(BF)


def spread_kernel(chosen_ref, ret_ref, out_ref):
    tile = out_ref.shape[0]
    column = slot_column(chosen_ref[0].astype(F32)).astype(jnp.int32) - pl.program_id(0) * tile
    lanes = lax.broadcasted_iota(jnp.int32, (column.shape[0], tile), 1)
    hot = jnp.where(lanes == column, jnp.float32(1.0), jnp.float32(0.0)).astype(BF)
    out_ref[...] = lax.dot_general(
        hot, ret_ref[...], (((0,), (0,)), ((), ())), preferred_element_type=F32
    ).astype(BF)


def spread_rows(chosen, ret, length):
    rows, width = ret.shape
    tile = 256
    return pl.pallas_call(
        spread_kernel,
        grid=(length // tile,),
        in_specs=[
            pl.BlockSpec(chosen.shape, lambda i: (0, 0, 0)),
            pl.BlockSpec((rows, width), lambda i: (0, 0)),
        ],
        out_specs=pl.BlockSpec((tile, width), lambda i: (i, 0)),
        out_shape=jax.ShapeDtypeStruct((length, width), BF),
        name="spread_rows",
    )(chosen, ret)


OWN, YY, ZM, ZP, OO, OY, MY, PY = range(8)
PIECE_M, PIECE_P, PIECE_Y, PIECE_A, PIECE_B, PIECE_OY, PIECE_MY, PIECE_PY = range(8)
RS_Y1, RS_A, RS_B, RS_LM, RS_LP, RS_M0, RS_M1, RS_P0, RS_P1, RS_Y = range(10)
CH = 64
HALF = CH // 2
SL = 16


def layer_kernel(
    chosen_ref,
    counts_ref,
    gates_ref,
    tok_hbm,
    cot_hbm,
    win_hbm,
    wout_hbm,
    ret_ref,
    dwin_hbm,
    dwout_hbm,
    px,
    pg,
    hot,
    xbuf,
    gbuf,
    win,
    wout,
    act_t,
    hg_t,
    slope_buf,
    sg,
    pair,
    rs_y1,
    rs_half,
    rs_leaf,
    rs_last,
    fin,
    back,
    tile_in,
    tile_out,
    tok_sem,
    a_send,
    a_recv,
    own_sem,
    w_sem,
    ag_send,
    ag_recv,
    core_send,
    core_recv,
    pr_send,
    pr_recv,
    rs_send,
    rs_recv,
    d_send,
    d_recv,
    t_sem,
):
    g = lax.axis_index("group")
    f = lax.axis_index("fsdp")
    h, x = g // 4, lax.rem(g, 4)
    z, l, c = f // 4, lax.rem(f // 2, 2), lax.rem(f, 2)
    up, down, far = lax.rem(z + 1, 4), lax.rem(z + 3, 4), lax.rem(z + 2, 4)
    unit_of = {
        OWN: z * 2 + l,
        YY: z * 2 + (1 - l),
        ZM: down * 2 + l,
        ZP: up * 2 + l,
        OO: far * 2 + l,
        OY: far * 2 + (1 - l),
        MY: down * 2 + (1 - l),
        PY: up * 2 + (1 - l),
    }
    to_up, to_down = up * 4 + l * 2 + c, down * 4 + l * 2 + c
    to_y = z * 4 + (1 - l) * 2 + c
    to_core = z * 4 + l * 2 + (1 - c)
    batch_rows = 16 * CH

    hops = [(0, 1), (0, 2), (0, 3), (1, 0), (1, 1), (1, 2), (1, 3)]

    def partner(b, k):
        px_ = lax.rem(x + k, 4)
        return (h * 4 + px_, f) if b == 0 else ((1 - h) * 4 + px_, to_y)

    def source_x(k):
        return lax.rem(x + 4 - k, 4)

    def ds(start, size):
        return pl.ds(pl.multiple_of(start, 16), size)

    def chunk(b, u, which):
        return b * batch_rows + (unit_of[u] * 2 + which) * CH

    def mine(b, u, start=0, size=CH):
        return ds(chunk(b, u, c) + start, size)

    def other(b, u):
        return ds(chunk(b, u, 1 - c), CH)

    def unit_rows(b, u):
        return pl.ds(pl.multiple_of(b * batch_rows + unit_of[u] * 2 * CH, 2 * CH), 2 * CH)

    length = tok_hbm.shape[0]
    width = tok_hbm.shape[1]
    token_copies = []
    for a, source in enumerate((tok_hbm, cot_hbm)):
        for j in range(4):
            cols = pl.ds(j * (width // 4), width // 4)
            copy = pltpu.make_async_copy(
                source.at[:, cols], sg.at[pl.ds(a * length, length), cols], tok_sem.at[a, j]
            )
            copy.start()
            token_copies.append(copy)
    w_copies = [
        pltpu.make_async_copy(win_hbm.at[0], win, w_sem.at[0]),
        pltpu.make_async_copy(wout_hbm.at[0], wout, w_sem.at[1]),
    ]
    for w in w_copies:
        w.start()
    barrier = pltpu.get_barrier_semaphore()
    for b, k in hops:
        pl.semaphore_signal(barrier, inc=1, device_id=partner(b, k), device_id_type=MESH)
    for d in (to_up, to_down, to_y, to_core):
        pl.semaphore_signal(barrier, inc=1, device_id=(g, d), device_id_type=MESH)

    hot[...] = one_hot_rows(chosen_ref[0], length)
    slot_iota = lax.broadcasted_iota(jnp.int32, chosen_ref.shape[1:], 1)
    experts = chosen_ref.shape[1]
    lane = lax.broadcasted_iota(jnp.int32, (experts, experts), 1)
    row = lax.broadcasted_iota(jnp.int32, (experts, experts), 0)
    limit = jnp.sum(
        jnp.where(lane == row, jnp.broadcast_to(counts_ref[...].astype(F32), (experts, experts)), 0.0),
        axis=1,
        keepdims=True,
    )
    live = jnp.where(slot_iota.astype(F32) < limit, gates_ref[0], jnp.float32(0.0))
    gate = slot_column(live)

    bufs = (xbuf, gbuf)
    picked = (px, pg)
    pending = []

    def start(copy):
        copy.start()
        pending.append(copy)

    def remote(src, dst, send, recv, dest):
        return pltpu.make_async_remote_copy(
            src_ref=src, dst_ref=dst, send_sem=send, recv_sem=recv, device_id=dest, device_id_type=MESH
        )

    def a_start(a, i):
        b, k = hops[i]
        dest = partner(b, k)
        start(
            remote(
                picked[a].at[ds(dest[0] * SL, SL)],
                bufs[a].at[ds(b * batch_rows + dest[1] * CH + x * SL, SL)],
                a_send.at[a, i],
                a_recv.at[a, i],
                dest,
            )
        )

    def a_wait(a, batch):
        for i, (b, k) in enumerate(hops):
            if b == batch:
                here = bufs[a].at[ds(b * batch_rows + f * CH + source_x(k) * SL, SL)]
                remote(here, here, a_send.at[a, i], a_recv.at[a, i], (g, to_y)).wait_recv()

    own_copies = []
    for a in range(2):
        for j in range(4):
            cols = pl.ds(j * (width // 4), width // 4)
            token_copies[a * 4 + j].wait()
            rows = jnp.dot(hot[...], sg[pl.ds(a * length, length), cols], preferred_element_type=F32)
            picked[a][:, cols] = (rows if a == 0 else gate * rows).astype(BF)
        if a == 0:
            pl.semaphore_wait(barrier, len(hops) + 4)
        for i in range(3):
            a_start(a, i)
        own = pltpu.make_async_copy(
            picked[a].at[ds(g * SL, SL)], bufs[a].at[ds(f * CH + x * SL, SL)], own_sem.at[a]
        )
        own.start()
        own_copies.append(own)
        if a == 1:
            for aa in range(2):
                for i in range(3, 7):
                    a_start(aa, i)

    def ag(a, b, rows, dest, piece):
        return remote(
            bufs[a].at[rows], bufs[a].at[rows], ag_send.at[a, b, piece], ag_recv.at[a, b, piece], (g, dest)
        )

    def ag_wait(a, b, rows, piece):
        ag(a, b, rows, to_y, piece).wait_recv()

    def core(a, b, u, rows):
        return remote(
            bufs[a].at[rows], bufs[a].at[rows], core_send.at[a, b, u], core_recv.at[a, b, u], (g, to_core)
        )

    def core_start(a, b, u):
        start(core(a, b, u, mine(b, u)))

    def core_wait(a, b, u):
        core(a, b, u, other(b, u)).wait_recv()

    def rows_of(ref, b, us):
        return jnp.concatenate([ref[unit_rows(b, u), :] for u in us], axis=0)

    def forward(b, us):
        for u in us:
            core_wait(0, b, u)
        hidden = jnp.dot(rows_of(xbuf, b, us), win[...], preferred_element_type=F32)
        activation, slope = gelu_parts(hidden)
        turned = activation.T.astype(BF)
        for i, u in enumerate(us):
            part = slice(i * 2 * CH, (i + 1) * 2 * CH)
            act_t[:, unit_rows(b, u)] = turned[:, part]
            slope_buf[unit_rows(b, u), :] = slope[part, :]

    def pair_copy(b, u, rows):
        return remote(
            sg.at[rows], pair.at[b, unit_of[u]], pr_send.at[b, u], pr_recv.at[b, u], (g, to_core)
        )

    def backward(b, us):
        for u in us:
            core_wait(1, b, u)
        back_hidden = lax.dot_general(
            rows_of(gbuf, b, us), wout[...], (((1,), (1,)), ((), ())), preferred_element_type=F32
        )
        hidden_grad = back_hidden * rows_of(slope_buf, b, us)
        turned = hidden_grad.T.astype(BF)
        for i, u in enumerate(us):
            hg_t[:, unit_rows(b, u)] = turned[:, i * 2 * CH : (i + 1) * 2 * CH]
        hidden_grad = hidden_grad.astype(BF)

        @pl.loop(0, 4)
        def _(j):
            cols = pl.ds(pl.multiple_of(j * 512, 512), 512)
            part = lax.dot_general(
                hidden_grad, win[cols, :], (((1,), (1,)), ((), ())), preferred_element_type=F32
            ).astype(BF)
            for i, u in enumerate(us):
                sg[unit_rows(b, u), cols] = part[i * 2 * CH : (i + 1) * 2 * CH, :]

        for u in us:
            start(pair_copy(b, u, other(b, u)))

    def accumulate(base, size, load):
        @pl.loop(0, size // 16)
        def _(i):
            rows = ds(base + i * 16, 16)
            total = sg[rows, :].astype(F32)
            sg[rows, :] = (total + load(ds(i * 16, 16))).astype(BF)

    def pair_add(b, u):
        pair_copy(b, u, mine(b, u)).wait_recv()
        slab = pair.at[b, unit_of[u]]
        accumulate(chunk(b, u, c), CH, lambda r: slab[r, :].astype(F32))

    def rs(b, rows, dst, idx, dest):
        return remote(sg.at[rows], dst, rs_send.at[b, idx], rs_recv.at[b, idx], (g, dest))

    def rs_start(b, rows, dst, idx, dest):
        start(rs(b, rows, dst, idx, dest))

    def rs_wait(b, dst, idx, size=CH):
        rs(b, mine(b, OWN, 0, size), dst, idx, to_y).wait_recv()

    def tile_copies(slot, j):
        cols = pl.ds(pl.multiple_of(j * 256, 256), 256)
        return (
            pltpu.make_async_copy(tile_in.at[slot], dwin_hbm.at[0, cols, :], t_sem.at[0, slot]),
            pltpu.make_async_copy(tile_out.at[slot], dwout_hbm.at[0, :, cols], t_sem.at[1, slot]),
        )

    def weight_tiles(first, last):
        @pl.loop(first, last)
        def _(j):
            slot = lax.rem(j, 2)
            cols = pl.ds(pl.multiple_of(j * 256, 256), 256)
            into, outof = tile_copies(slot, j)

            @pl.when(j >= 2)
            def _():
                into.wait()
                outof.wait()

            tile_in[slot] = jnp.dot(hg_t[...], xbuf[:, cols], preferred_element_type=F32).T
            into.start()
            tile_out[slot] = jnp.dot(act_t[...], gbuf[:, cols], preferred_element_type=F32)
            outof.start()

    def own_out(b):
        for a in range(2):
            if b == 0:
                own_copies[a].wait()
            a_wait(a, b)
            start(ag(a, b, mine(b, OWN), to_up, PIECE_M))
            start(ag(a, b, mine(b, OWN), to_down, PIECE_P))
            start(ag(a, b, mine(b, OWN), to_y, PIECE_Y))
            core_start(a, b, OWN)

    def near(a, b):
        ag_wait(a, b, mine(b, ZM), PIECE_M)
        start(ag(a, b, mine(b, ZM, 0, HALF), to_up, PIECE_A))
        core_start(a, b, ZM)
        ag_wait(a, b, mine(b, ZP), PIECE_P)
        start(ag(a, b, mine(b, ZP, HALF, HALF), to_down, PIECE_B))
        core_start(a, b, ZP)

    def side_wait(a, b):
        ag_wait(a, b, mine(b, YY), PIECE_Y)
        core_start(a, b, YY)

    def side_out(a, b):
        start(ag(a, b, mine(b, YY), to_up, PIECE_MY))
        start(ag(a, b, mine(b, YY), to_down, PIECE_PY))

    def far_out(a, b):
        ag_wait(a, b, mine(b, OO, 0, HALF), PIECE_A)
        ag_wait(a, b, mine(b, OO, HALF, HALF), PIECE_B)
        start(ag(a, b, mine(b, OO), to_y, PIECE_OY))
        core_start(a, b, OO)

    def land(a, b, u, piece):
        ag_wait(a, b, mine(b, u), piece)
        core_start(a, b, u)

    def leaves(b):
        pair_add(b, MY)
        rs_start(b, mine(b, MY), rs_leaf.at[b, 1], RS_LP, to_down)
        pair_add(b, PY)
        rs_start(b, mine(b, PY), rs_leaf.at[b, 0], RS_LM, to_up)

    def y_leaf(b):
        pair_add(b, OY)
        rs_start(b, mine(b, OY), rs_y1.at[b], RS_Y1, to_y)

    def far_sum(b):
        pair_add(b, OO)
        rs_wait(b, rs_y1.at[b], RS_Y1)
        accumulate(chunk(b, OO, c), CH, lambda r: rs_y1[b, r, :].astype(F32))
        rs_start(b, mine(b, OO, 0, HALF), rs_half.at[b, 0], RS_A, to_down)
        rs_start(b, mine(b, OO, HALF, HALF), rs_half.at[b, 1], RS_B, to_up)

    def near_free(b):
        rs_start(b, mine(b, ZM, HALF, HALF), rs_last.at[b, 1, pl.ds(HALF, HALF)], RS_P1, to_down)
        rs_start(b, mine(b, ZP, 0, HALF), rs_last.at[b, 0, pl.ds(0, HALF)], RS_M0, to_up)

    def near_sum(b):
        rs_wait(b, rs_half.at[b, 0], RS_A, HALF)
        accumulate(chunk(b, ZM, c), HALF, lambda r: rs_half[b, 0, r, :].astype(F32))
        rs_start(b, mine(b, ZM, 0, HALF), rs_last.at[b, 1, pl.ds(0, HALF)], RS_P0, to_down)
        rs_wait(b, rs_half.at[b, 1], RS_B, HALF)
        accumulate(chunk(b, ZP, c) + HALF, HALF, lambda r: rs_half[b, 1, r, :].astype(F32))
        rs_start(b, mine(b, ZP, HALF, HALF), rs_last.at[b, 0, pl.ds(HALF, HALF)], RS_M1, to_up)

    def side_sum(b):
        rs_wait(b, rs_leaf.at[b, 0], RS_LM)
        rs_wait(b, rs_leaf.at[b, 1], RS_LP)
        accumulate(
            chunk(b, YY, c),
            CH,
            lambda r: rs_leaf[b, 0, r, :].astype(F32) + rs_leaf[b, 1, r, :].astype(F32),
        )
        rs_start(b, mine(b, YY), rs_last.at[b, 2], RS_Y, to_y)

    def d_copy(i):
        b, k = hops[i]
        dest = partner(b, k)
        return remote(
            fin.at[ds(b * CH + lax.rem(x + k, 4) * SL, SL)],
            back.at[ds(g * SL, SL)],
            d_send.at[i],
            d_recv.at[i],
            dest,
        )

    def finish(b):
        rs_wait(b, rs_last.at[b, 0, pl.ds(0, HALF)], RS_M0, HALF)
        rs_wait(b, rs_last.at[b, 0, pl.ds(HALF, HALF)], RS_M1, HALF)
        rs_wait(b, rs_last.at[b, 1, pl.ds(0, HALF)], RS_P0, HALF)
        rs_wait(b, rs_last.at[b, 1, pl.ds(HALF, HALF)], RS_P1, HALF)
        rs_wait(b, rs_last.at[b, 2], RS_Y)

        @pl.loop(0, CH // 16)
        def _(i):
            rows = ds(chunk(b, OWN, c) + i * 16, 16)
            r = ds(i * 16, 16)
            total = sg[rows, :].astype(F32) + rs_last[b, 0, r, :].astype(F32)
            total = total + rs_last[b, 1, r, :].astype(F32) + rs_last[b, 2, r, :].astype(F32)
            fin[ds(b * CH + i * 16, 16), :] = total.astype(BF)

        for i in range(len(hops)):
            if hops[i][0] == b:
                start(d_copy(i))

    own_out(0)
    for w in w_copies:
        w.wait()
    near(0, 0)
    side_wait(0, 0)
    forward(0, (ZM, ZP))
    near(1, 0)
    side_out(0, 0)
    side_wait(1, 0)
    side_out(1, 0)
    forward(0, (OWN, YY))
    backward(0, (ZM, ZP))
    far_out(0, 0)
    backward(0, (OWN, YY))
    far_out(1, 0)
    own_out(1)
    for u in (ZM, ZP, OWN, YY):
        pair_add(0, u)
    land(0, 0, OY, PIECE_OY)
    forward(0, (OO, OY))
    land(0, 0, MY, PIECE_MY)
    land(0, 0, PY, PIECE_PY)
    forward(0, (MY, PY))
    land(1, 0, OY, PIECE_OY)
    backward(0, (OO, OY))
    land(1, 0, MY, PIECE_MY)
    land(1, 0, PY, PIECE_PY)
    y_leaf(0)
    backward(0, (MY, PY))
    leaves(0)

    near(0, 1)
    side_wait(0, 1)
    forward(1, (ZM, ZP))
    near(1, 1)
    side_out(0, 1)
    side_wait(1, 1)
    side_out(1, 1)
    far_sum(0)
    near_free(0)
    forward(1, (OWN, YY))
    backward(1, (ZM, ZP))
    far_out(0, 1)
    backward(1, (OWN, YY))
    far_out(1, 1)
    side_sum(0)
    for u in (ZM, ZP, OWN, YY):
        pair_add(1, u)
    land(0, 1, OY, PIECE_OY)
    forward(1, (OO, OY))
    land(0, 1, MY, PIECE_MY)
    land(0, 1, PY, PIECE_PY)
    forward(1, (MY, PY))
    land(1, 1, OY, PIECE_OY)
    backward(1, (OO, OY))
    y_leaf(1)
    land(1, 1, MY, PIECE_MY)
    land(1, 1, PY, PIECE_PY)
    backward(1, (MY, PY))
    leaves(1)
    near_sum(0)
    near_free(1)
    weight_tiles(0, 2)
    far_sum(1)
    finish(0)
    weight_tiles(2, 4)
    side_sum(1)
    near_sum(1)
    weight_tiles(4, 8)
    finish(1)
    own_rows = ds(g * SL, SL)
    back[own_rows, :] = fin[ds(x * SL, SL), :]
    for slot in range(2):
        into, outof = tile_copies(slot, 6 + slot)
        into.wait()
        outof.wait()
    for i, (b, k) in enumerate(hops):
        sender = (h if b == 0 else 1 - h) * 4 + source_x(k)
        remote(
            fin.at[pl.ds(0, SL)], back.at[ds(sender * SL, SL)], d_send.at[i], d_recv.at[i], (g, to_y)
        ).wait_recv()
    ret_ref[...] = back[...]
    for copy in pending:
        copy.wait_send()


def layer(chosen, counts, gates, tokens_in, out_grad, w_in, w_out):
    width = tokens_in.shape[1]
    hidden = w_in.shape[2]
    rows = chosen.shape[1] * chosen.shape[2]
    total = rows * lax.axis_size("fsdp")
    vmem, dma = pltpu.VMEM, pltpu.SemaphoreType.DMA
    in_vmem, in_hbm = pl.BlockSpec(memory_space=pltpu.VMEM), pl.BlockSpec(memory_space=pl.ANY)
    return pl.pallas_call(
        layer_kernel,
        out_shape=[
            jax.ShapeDtypeStruct((rows, width), BF),
            jax.ShapeDtypeStruct((1, width, hidden), F32),
            jax.ShapeDtypeStruct((1, hidden, width), F32),
        ],
        in_specs=[in_vmem] * 3 + [in_hbm] * 4,
        out_specs=[in_vmem, in_hbm, in_hbm],
        scratch_shapes=[
            vmem((rows, width), BF),
            vmem((rows, width), BF),
            vmem((rows, tokens_in.shape[0]), BF),
            vmem((total, width), BF),
            vmem((total, width), BF),
            vmem((width, hidden), BF),
            vmem((hidden, width), BF),
            vmem((hidden, total), BF),
            vmem((hidden, total), BF),
            vmem((total, hidden), F32),
            vmem((total, width), BF),
            vmem((2, 8, CH, width), BF),
            vmem((2, CH, width), BF),
            vmem((2, 2, HALF, width), BF),
            vmem((2, 2, CH, width), BF),
            vmem((2, 3, CH, width), BF),
            vmem((rows, width), BF),
            vmem((rows, width), BF),
            vmem((2, 256, hidden), F32),
            vmem((2, hidden, 256), F32),
            dma((2, 4)),
            dma((2, 7)),
            dma((2, 7)),
            dma((2,)),
            dma((2,)),
            dma((2, 2, 8)),
            dma((2, 2, 8)),
            dma((2, 2, 8)),
            dma((2, 2, 8)),
            dma((2, 8)),
            dma((2, 8)),
            dma((2, 10)),
            dma((2, 10)),
            dma((7,)),
            dma((7,)),
            dma((2, 2)),
        ],
        compiler_params=pltpu.CompilerParams(
            collective_id=0, has_side_effects=True, vmem_limit_bytes=62 * 1024 * 1024
        ),
        name="layer",
    )(chosen, counts, gates, tokens_in, out_grad, w_in, w_out)


def shards(tokens_in, out_grad, w_in, w_out, chosen, counts, gates):
    ret, grad_w_in, grad_w_out = layer(chosen, counts, gates, tokens_in, out_grad, w_in, w_out)
    grad_in = spread_rows(chosen, ret, tokens_in.shape[0])
    return (grad_in, grad_w_in, grad_w_out)


def solution(mesh):
    placed = (
        P(("group", "fsdp"), None),
        P(("group", "fsdp"), None),
        P("group", None, "fsdp"),
        P("group", "fsdp", None),
        P(("group", "fsdp"), None, None),
        P(("group", "fsdp"), None),
        P(("group", "fsdp"), None, None),
    )
    return jax.shard_map(
        shards,
        mesh=mesh,
        in_specs=placed,
        out_specs=(P(("group", "fsdp"), None), P("group", None, "fsdp"), P("group", "fsdp", None)),
        check_vma=False,
    )
```

time: 404 us -> 134 us (0.33)
  waiting for transfers between devices: 256 us -> 0 us
  Pallas kernels: 0 us -> 125 us
  matrix products: 49.9 us -> 0 us
  blocking collectives: 31.9 us -> 0 us
  local copies, waits for them, and re-layouts: 29.6 us -> 6.83 us
  between operations: 13.9 us -> 0.64 us
  other arithmetic: 12.4 us -> 0 us
  starting transfers between devices: 7.07 us -> 0 us
    reduce_scatter x1 -> x0, waiting for transfers between devices: 172 us -> none  [shards(): lax.psum_scatter(partial_grad, 'fsdp', scatter_dimension=0, tiled=True)]
    pallas_call x0 -> x2, Pallas kernels: none -> 125 us  [the longest x1 120 us: layer(): pl.pallas_call(layer_kernel, out_shape=[jax.ShapeDtypeStruct((rows, width...]
    all_gather x2 -> x0, waiting for transfers between devices: 82.7 us -> none  [the longest x1 46.4 us: shards(): lax.all_gather(near_grad, 'fsdp', axis=0, tiled=True)]
    dot_general x5 -> x0, matrix products: 49.9 us -> none  [the longest x1 12.1 us: shards(): lax.dot_general(expert_grad, w_out[0], (((1,), (1,)), ((), ())), preferre...]
    all_to_all x2 -> x0, blocking collectives: 31.9 us -> none  [the longest x1 16.3 us: shards(): lax.all_to_all(picked_x, 'group', split_axis=0, concat_axis=0, tiled=True)]
    transpose x1 -> x0, local copies, waits for them, and re-layouts: 19.4 us -> none  [shards(): jnp.einsum('secf,edf->secd', stacked_grad, w_in, preferred_element_type=j...]
    gather x2 -> x0, local copies, waits for them, and re-layouts: 8.34 us -> none  [the longest x1 4.17 us: shards(): jnp.take(out_grad, slot_rows, axis=0).astype(jnp.float32)]
    all_to_all x1 -> x0, starting transfers between devices: 6.94 us -> none  [shards(): lax.all_to_all(shares.reshape(group_count, exp_local, slot_count, model_w...]
  transfers between devices with their start and end apart: 4 -> 0, of which waited for: 4 -> 0; matrix products, arithmetic and copies ran while one was open for 9% -> 0% of each run, Pallas kernels for 0% -> 0%
where the time goes in v2:
time: 134 us; the launch traced here: 132 us
  Pallas kernels  125 us (93%)
  local copies, waits for them, and re-layouts  6.83 us (5%)
    pallas_call x1, Pallas kernels, layer(): pl.pallas_call(layer_kernel, out_shape=[jax.ShapeDtypeStruct((rows, width...  120 us
    unnamed x4, local copies, waits for them, and re-layouts  6.83 us
    pallas_call x1, Pallas kernels, spread_rows(): pl.pallas_call(spread_kernel, grid=(length // tile,), in_specs=[pl.BlockS...  4.67 us

profile of v2, /device:TPU:4, one launch (start us, length us, event | category | flops | bytes accessed | tf_op | source)
XLA Modules:
  0.0 132.4 jit_solution(332022125489039199)
XLA Ops:
  0.6 120.2 %layer.1 = (bf16[128,2048]{1,0:T(8,128)(2,1)}, f32[1,2048,512]{2,1,0:T(8,128)}, f32[1,512,2048]{2,1,0:T(8,128)}) custom-call(s32[1,8,16]{2,1,0:T(8,128)} %chosen_ref.3, s32[1,8]{1,0:T(1,128)} %counts_ref.1, f32[1,8,16]{2,1,0:T(8,128)} %gates_ref.1, bf16[1024,2048]{1,0:T(8,128)(2,1)} %tok_hbm.1, bf16[1024,2048]{1,0:T(8,128)(2,1)} %cot_hbm.1, ...), custom_call_target="tpu_custom_call" | custom-call | tf_op jit(solution)/shard_map/layer/pallas_call | solution.py:561
  120.9 4.7 %spread_rows.1 = bf16[1024,2048]{1,0:T(8,128)(2,1)} custom-call(s32[1,8,16]{2,1,0:T(8,128)} %chosen_ref.3, bf16[128,2048]{1,0:T(8,128)(2,1)} %get-tuple-element.6.ret_ref), custom_call_target="tpu_custom_call" | custom-call | tf_op jit(solution)/shard_map/spread_rows/pallas_call | solution.py:54
  125.5 0.0 copy-start
  125.5 4.8 %copy.12 = f32[1,2048,512]{2,1,0:T(8,128)} copy(f32[1,2048,512]{2,1,0:T(8,128)} %get-tuple-element.13) | data formatting | bytes 8388608
  130.4 0.0 copy-done
  130.4 2.0 %copy.13 = f32[1,512,2048]{2,1,0:T(8,128)} copy(f32[1,512,2048]{2,1,0:T(8,128)S(1)} %copy-done) | data formatting | bytes 8388608
Async XLA Ops:
  125.5 4.8 %copy-start = (f32[1,512,2048]{2,1,0:T(8,128)S(1)}, f32[1,512,2048]{2,1,0:T(8,128)}, u32[]{:S(2)}) copy-start(f32[1,512,2048]{2,1,0:T(8,128)} %get-tuple-element.14) | copy-start | bytes 12582916

commit v3 on v2

--- a/solution.py
+++ b/solution.py
@@ -38,38 +38,69 @@
     return jnp.where(lanes == column, jnp.float32(1.0), jnp.float32(0.0)).astype(BF)
 
 
-def spread_kernel(chosen_ref, ret_ref, out_ref):
-    tile = out_ref.shape[0]
-    column = slot_column(chosen_ref[0].astype(F32)).astype(jnp.int32) - pl.program_id(0) * tile
-    lanes = lax.broadcasted_iota(jnp.int32, (column.shape[0], tile), 1)
-    hot = jnp.where(lanes == column, jnp.float32(1.0), jnp.float32(0.0)).astype(BF)
-    out_ref[...] = lax.dot_general(
-        hot, ret_ref[...], (((0,), (0,)), ((), ())), preferred_element_type=F32
-    ).astype(BF)
-
-
-def spread_rows(chosen, ret, length):
+def spread_kernel(chosen_ref, ret_ref, dwin_ref, dwout_ref, out_hbm, win_hbm, wout_hbm, tiles, sem):
+    copies = [
+        pltpu.make_async_copy(dwin_ref, win_hbm.at[0], sem.at[0]),
+        pltpu.make_async_copy(dwout_ref, wout_hbm.at[0], sem.at[1]),
+    ]
+    for copy in copies:
+        copy.start()
+    count, size = tiles.shape[0], tiles.shape[1]
+    column = slot_column(chosen_ref[0].astype(F32)).astype(jnp.int32)
+    lanes = lax.broadcasted_iota(jnp.int32, (column.shape[0], size), 1)
+    for i in range(count):
+        hot = jnp.where(lanes + i * size == column, jnp.float32(1.0), jnp.float32(0.0)).astype(BF)
+        tiles[i] = lax.dot_general(
+            hot, ret_ref[...], (((0,), (0,)), ((), ())), preferred_element_type=F32
+        ).astype(BF)
+        copy = pltpu.make_async_copy(tiles.at[i], out_hbm.at[pl.ds(i * size, size)], sem.at[2 + i])
+        copy.start()
+        copies.append(copy)
+    for copy in copies:
+        copy.wait()
+
+
+def spread_rows(chosen, ret, dwin, dwout, length):
     rows, width = ret.shape
-    tile = 256
+    count = 4
+    in_vmem, in_hbm = pl.BlockSpec(memory_space=pltpu.VMEM), pl.BlockSpec(memory_space=pltpu.HBM)
     return pl.pallas_call(
         spread_kernel,
-        grid=(length // tile,),
-        in_specs=[
-            pl.BlockSpec(chosen.shape, lambda i: (0, 0, 0)),
-            pl.BlockSpec((rows, width), lambda i: (0, 0)),
+        in_specs=[in_vmem] * 4,
+        out_specs=[in_hbm] * 3,
+        out_shape=[
+            jax.ShapeDtypeStruct((length, width), BF),
+            jax.ShapeDtypeStruct((1,) + dwin.shape, F32),
+            jax.ShapeDtypeStruct((1,) + dwout.shape, F32),
         ],
-        out_specs=pl.BlockSpec((tile, width), lambda i: (i, 0)),
-        out_shape=jax.ShapeDtypeStruct((length, width), BF),
+        scratch_shapes=[
+            pltpu.VMEM((count, length // count, width), BF),
+            pltpu.SemaphoreType.DMA((2 + count,)),
+        ],
+        compiler_params=pltpu.CompilerParams(vmem_limit_bytes=12 * 1024 * 1024),
         name="spread_rows",
-    )(chosen, ret)
+    )(chosen, ret, dwin, dwout)
 
 
 OWN, YY, ZM, ZP, OO, OY, MY, PY = range(8)
-PIECE_M, PIECE_P, PIECE_Y, PIECE_A, PIECE_B, PIECE_OY, PIECE_MY, PIECE_PY = range(8)
-RS_Y1, RS_A, RS_B, RS_LM, RS_LP, RS_M0, RS_M1, RS_P0, RS_P1, RS_Y = range(10)
+PIECE_M, PIECE_P, PIECE_Y, PIECE_A, PIECE_B, PIECE_OY, PIECE_MY, PIECE_PY, PIECE_QM, PIECE_QP = range(10)
+RS_Y1, RS_A, RS_B, RS_LM, RS_LP, RS_M0, RS_M1, RS_P0, RS_P1, RS_Y, RS_QM, RS_QP = range(12)
 CH = 64
+LAYER_VMEM = 52 * 1024 * 1024
 HALF = CH // 2
 SL = 16
+QS = 16
+PLACE = {
+    (0, 0): (0, 0),
+    (0, 1): (0, 1),
+    (1, 0): (0, 2),
+    (1, 1): (0, 3),
+    (0, 2): (1, 0),
+    (0, 3): (1, 1),
+    (1, 2): (1, 2),
+    (1, 3): (1, 3),
+}
+HOPS = [hop for hop in PLACE if hop != (0, 0)]
 
 
 def layer_kernel(
@@ -81,8 +112,8 @@
     win_hbm,
     wout_hbm,
     ret_ref,
-    dwin_hbm,
-    dwout_hbm,
+    dwin_ref,
+    dwout_ref,
     px,
     pg,
     hot,
@@ -99,10 +130,9 @@
     rs_half,
     rs_leaf,
     rs_last,
+    rs_q,
     fin,
     back,
-    tile_in,
-    tile_out,
     tok_sem,
     a_send,
     a_recv,
@@ -118,7 +148,6 @@
     rs_recv,
     d_send,
     d_recv,
-    t_sem,
 ):
     g = lax.axis_index("group")
     f = lax.axis_index("fsdp")
@@ -140,14 +169,10 @@
     to_core = z * 4 + l * 2 + (1 - c)
     batch_rows = 16 * CH
 
-    hops = [(0, 1), (0, 2), (0, 3), (1, 0), (1, 1), (1, 2), (1, 3)]
-
-    def partner(b, k):
-        px_ = lax.rem(x + k, 4)
-        return (h * 4 + px_, f) if b == 0 else ((1 - h) * 4 + px_, to_y)
-
-    def source_x(k):
-        return lax.rem(x + 4 - k, 4)
+    def partner(flip, k):
+        if flip:
+            return ((1 - h) * 4 + lax.rem(x + k, 4), to_y)
+        return (h * 4 + lax.rem(x + k, 4), f)
 
     def ds(start, size):
         return pl.ds(pl.multiple_of(start, 16), size)
@@ -182,8 +207,8 @@
     for w in w_copies:
         w.start()
     barrier = pltpu.get_barrier_semaphore()
-    for b, k in hops:
-        pl.semaphore_signal(barrier, inc=1, device_id=partner(b, k), device_id_type=MESH)
+    for hop in HOPS:
+        pl.semaphore_signal(barrier, inc=1, device_id=partner(*hop), device_id_type=MESH)
     for d in (to_up, to_down, to_y, to_core):
         pl.semaphore_signal(barrier, inc=1, device_id=(g, d), device_id_type=MESH)
 
@@ -213,23 +238,26 @@
             src_ref=src, dst_ref=dst, send_sem=send, recv_sem=recv, device_id=dest, device_id_type=MESH
         )
 
-    def a_start(a, i):
-        b, k = hops[i]
-        dest = partner(b, k)
-        start(
-            remote(
-                picked[a].at[ds(dest[0] * SL, SL)],
-                bufs[a].at[ds(b * batch_rows + dest[1] * CH + x * SL, SL)],
-                a_send.at[a, i],
-                a_recv.at[a, i],
-                dest,
-            )
-        )
+    def a_start(a, batch):
+        for i, hop in enumerate(HOPS):
+            b, place = PLACE[hop]
+            if b == batch:
+                dest = partner(*hop)
+                start(
+                    remote(
+                        picked[a].at[ds(dest[0] * SL, SL)],
+                        bufs[a].at[ds(b * batch_rows + dest[1] * CH + place * SL, SL)],
+                        a_send.at[a, i],
+                        a_recv.at[a, i],
+                        dest,
+                    )
+                )
 
     def a_wait(a, batch):
-        for i, (b, k) in enumerate(hops):
+        for i, hop in enumerate(HOPS):
+            b, place = PLACE[hop]
             if b == batch:
-                here = bufs[a].at[ds(b * batch_rows + f * CH + source_x(k) * SL, SL)]
+                here = bufs[a].at[ds(b * batch_rows + f * CH + place * SL, SL)]
                 remote(here, here, a_send.at[a, i], a_recv.at[a, i], (g, to_y)).wait_recv()
 
     own_copies = []
@@ -240,18 +268,15 @@
             rows = jnp.dot(hot[...], sg[pl.ds(a * length, length), cols], preferred_element_type=F32)
             picked[a][:, cols] = (rows if a == 0 else gate * rows).astype(BF)
         if a == 0:
-            pl.semaphore_wait(barrier, len(hops) + 4)
-        for i in range(3):
-            a_start(a, i)
+            pl.semaphore_wait(barrier, len(HOPS) + 4)
+        a_start(a, 0)
         own = pltpu.make_async_copy(
-            picked[a].at[ds(g * SL, SL)], bufs[a].at[ds(f * CH + x * SL, SL)], own_sem.at[a]
+            picked[a].at[ds(g * SL, SL)], bufs[a].at[ds(f * CH, SL)], own_sem.at[a]
         )
         own.start()
         own_copies.append(own)
-        if a == 1:
-            for aa in range(2):
-                for i in range(3, 7):
-                    a_start(aa, i)
+    for a in range(2):
+        a_start(a, 1)
 
     def ag(a, b, rows, dest, piece):
         return remote(
@@ -336,29 +361,20 @@
     def rs_wait(b, dst, idx, size=CH):
         rs(b, mine(b, OWN, 0, size), dst, idx, to_y).wait_recv()
 
-    def tile_copies(slot, j):
-        cols = pl.ds(pl.multiple_of(j * 256, 256), 256)
-        return (
-            pltpu.make_async_copy(tile_in.at[slot], dwin_hbm.at[0, cols, :], t_sem.at[0, slot]),
-            pltpu.make_async_copy(tile_out.at[slot], dwout_hbm.at[0, :, cols], t_sem.at[1, slot]),
-        )
-
-    def weight_tiles(first, last):
+    def weight_tiles(b, first, last):
+        rows = pl.ds(b * batch_rows, batch_rows)
+
         @pl.loop(first, last)
         def _(j):
-            slot = lax.rem(j, 2)
             cols = pl.ds(pl.multiple_of(j * 256, 256), 256)
-            into, outof = tile_copies(slot, j)
-
-            @pl.when(j >= 2)
-            def _():
-                into.wait()
-                outof.wait()
-
-            tile_in[slot] = jnp.dot(hg_t[...], xbuf[:, cols], preferred_element_type=F32).T
-            into.start()
-            tile_out[slot] = jnp.dot(act_t[...], gbuf[:, cols], preferred_element_type=F32)
-            outof.start()
+            into = jnp.dot(hg_t[:, rows], xbuf[rows, cols], preferred_element_type=F32).T
+            outof = jnp.dot(act_t[:, rows], gbuf[rows, cols], preferred_element_type=F32)
+            if b == 0:
+                dwin_ref[cols, :] = into
+                dwout_ref[:, cols] = outof
+            else:
+                dwin_ref[cols, :] += into
+                dwout_ref[:, cols] += outof
 
     def own_out(b):
         for a in range(2):
@@ -377,14 +393,18 @@
         ag_wait(a, b, mine(b, ZP), PIECE_P)
         start(ag(a, b, mine(b, ZP, HALF, HALF), to_down, PIECE_B))
         core_start(a, b, ZP)
+        if a == 0:
+            start(ag(a, b, mine(b, ZM, 0, QS), to_y, PIECE_QM))
+            start(ag(a, b, mine(b, ZP, CH - QS, QS), to_y, PIECE_QP))
 
     def side_wait(a, b):
         ag_wait(a, b, mine(b, YY), PIECE_Y)
         core_start(a, b, YY)
 
     def side_out(a, b):
-        start(ag(a, b, mine(b, YY), to_up, PIECE_MY))
-        start(ag(a, b, mine(b, YY), to_down, PIECE_PY))
+        q = QS if a == 0 else 0
+        start(ag(a, b, mine(b, YY, q, CH - q), to_up, PIECE_MY))
+        start(ag(a, b, mine(b, YY, 0, CH - q), to_down, PIECE_PY))
 
     def far_out(a, b):
         ag_wait(a, b, mine(b, OO, 0, HALF), PIECE_A)
@@ -392,15 +412,27 @@
         start(ag(a, b, mine(b, OO), to_y, PIECE_OY))
         core_start(a, b, OO)
 
-    def land(a, b, u, piece):
-        ag_wait(a, b, mine(b, u), piece)
-        core_start(a, b, u)
+    def far_land(a, b):
+        ag_wait(a, b, mine(b, OY), PIECE_OY)
+        core_start(a, b, OY)
+
+    def side_land(a, b):
+        q = QS if a == 0 else 0
+        if q:
+            ag_wait(a, b, mine(b, MY, 0, q), PIECE_QM)
+            ag_wait(a, b, mine(b, PY, CH - q, q), PIECE_QP)
+        ag_wait(a, b, mine(b, MY, q, CH - q), PIECE_MY)
+        core_start(a, b, MY)
+        ag_wait(a, b, mine(b, PY, 0, CH - q), PIECE_PY)
+        core_start(a, b, PY)
 
     def leaves(b):
         pair_add(b, MY)
-        rs_start(b, mine(b, MY), rs_leaf.at[b, 1], RS_LP, to_down)
+        rs_start(b, mine(b, MY, QS, CH - QS), rs_leaf.at[b, 1, pl.ds(QS, CH - QS)], RS_LP, to_down)
+        rs_start(b, mine(b, MY, 0, QS), rs_q.at[b, 0], RS_QM, to_y)
         pair_add(b, PY)
-        rs_start(b, mine(b, PY), rs_leaf.at[b, 0], RS_LM, to_up)
+        rs_start(b, mine(b, PY, 0, CH - QS), rs_leaf.at[b, 0, pl.ds(0, CH - QS)], RS_LM, to_up)
+        rs_start(b, mine(b, PY, CH - QS, QS), rs_q.at[b, 1], RS_QP, to_y)
 
     def y_leaf(b):
         pair_add(b, OY)
@@ -418,32 +450,41 @@
         rs_start(b, mine(b, ZP, 0, HALF), rs_last.at[b, 0, pl.ds(0, HALF)], RS_M0, to_up)
 
     def near_sum(b):
+        rs_wait(b, rs_q.at[b, 0], RS_QM, QS)
+        accumulate(chunk(b, ZM, c), QS, lambda r: rs_q[b, 0, r, :].astype(F32))
         rs_wait(b, rs_half.at[b, 0], RS_A, HALF)
         accumulate(chunk(b, ZM, c), HALF, lambda r: rs_half[b, 0, r, :].astype(F32))
         rs_start(b, mine(b, ZM, 0, HALF), rs_last.at[b, 1, pl.ds(0, HALF)], RS_P0, to_down)
+        rs_wait(b, rs_q.at[b, 1], RS_QP, QS)
+        accumulate(chunk(b, ZP, c) + CH - QS, QS, lambda r: rs_q[b, 1, r, :].astype(F32))
         rs_wait(b, rs_half.at[b, 1], RS_B, HALF)
         accumulate(chunk(b, ZP, c) + HALF, HALF, lambda r: rs_half[b, 1, r, :].astype(F32))
         rs_start(b, mine(b, ZP, HALF, HALF), rs_last.at[b, 0, pl.ds(HALF, HALF)], RS_M1, to_up)
 
     def side_sum(b):
-        rs_wait(b, rs_leaf.at[b, 0], RS_LM)
-        rs_wait(b, rs_leaf.at[b, 1], RS_LP)
+        rs_wait(b, rs_leaf.at[b, 0, pl.ds(0, CH - QS)], RS_LM, CH - QS)
+        rs_wait(b, rs_leaf.at[b, 1, pl.ds(QS, CH - QS)], RS_LP, CH - QS)
+        base = chunk(b, YY, c)
+        low, high = rs_leaf.at[b, 0], rs_leaf.at[b, 1]
+        accumulate(base, QS, lambda r: low[r, :].astype(F32))
         accumulate(
-            chunk(b, YY, c),
-            CH,
-            lambda r: rs_leaf[b, 0, r, :].astype(F32) + rs_leaf[b, 1, r, :].astype(F32),
-        )
+            base + QS,
+            CH - 2 * QS,
+            lambda r: low.at[pl.ds(QS, CH - 2 * QS)][r, :].astype(F32)
+            + high.at[pl.ds(QS, CH - 2 * QS)][r, :].astype(F32),
+        )
+        accumulate(base + CH - QS, QS, lambda r: high.at[pl.ds(CH - QS, QS)][r, :].astype(F32))
         rs_start(b, mine(b, YY), rs_last.at[b, 2], RS_Y, to_y)
 
     def d_copy(i):
-        b, k = hops[i]
-        dest = partner(b, k)
+        flip, k = HOPS[i]
+        b, place = PLACE[HOPS[i]]
         return remote(
-            fin.at[ds(b * CH + lax.rem(x + k, 4) * SL, SL)],
+            fin.at[pl.ds(b * CH + place * SL, SL)],
             back.at[ds(g * SL, SL)],
             d_send.at[i],
             d_recv.at[i],
-            dest,
+            partner(flip, 4 - k),
         )
 
     def finish(b):
@@ -461,8 +502,8 @@
             total = total + rs_last[b, 1, r, :].astype(F32) + rs_last[b, 2, r, :].astype(F32)
             fin[ds(b * CH + i * 16, 16), :] = total.astype(BF)
 
-        for i in range(len(hops)):
-            if hops[i][0] == b:
+        for i, hop in enumerate(HOPS):
+            if PLACE[hop][0] == b:
                 start(d_copy(i))
 
     own_out(0)
@@ -476,22 +517,20 @@
     side_wait(1, 0)
     side_out(1, 0)
     forward(0, (OWN, YY))
+    far_out(0, 0)
     backward(0, (ZM, ZP))
-    far_out(0, 0)
-    backward(0, (OWN, YY))
     far_out(1, 0)
     own_out(1)
+    backward(0, (OWN, YY))
     for u in (ZM, ZP, OWN, YY):
         pair_add(0, u)
-    land(0, 0, OY, PIECE_OY)
+    far_land(0, 0)
     forward(0, (OO, OY))
-    land(0, 0, MY, PIECE_MY)
-    land(0, 0, PY, PIECE_PY)
+    side_land(0, 0)
     forward(0, (MY, PY))
-    land(1, 0, OY, PIECE_OY)
+    far_land(1, 0)
     backward(0, (OO, OY))
-    land(1, 0, MY, PIECE_MY)
-    land(1, 0, PY, PIECE_PY)
+    side_land(1, 0)
     y_leaf(0)
     backward(0, (MY, PY))
     leaves(0)
@@ -499,52 +538,49 @@
     near(0, 1)
     side_wait(0, 1)
     forward(1, (ZM, ZP))
+    weight_tiles(0, 0, 3)
     near(1, 1)
     side_out(0, 1)
     side_wait(1, 1)
     side_out(1, 1)
+    forward(1, (OWN, YY))
+    backward(1, (ZM, ZP))
     far_sum(0)
     near_free(0)
-    forward(1, (OWN, YY))
-    backward(1, (ZM, ZP))
+    weight_tiles(0, 3, 4)
     far_out(0, 1)
     backward(1, (OWN, YY))
     far_out(1, 1)
     side_sum(0)
     for u in (ZM, ZP, OWN, YY):
         pair_add(1, u)
-    land(0, 1, OY, PIECE_OY)
+    weight_tiles(0, 4, 7)
+    far_land(0, 1)
     forward(1, (OO, OY))
-    land(0, 1, MY, PIECE_MY)
-    land(0, 1, PY, PIECE_PY)
+    side_land(0, 1)
     forward(1, (MY, PY))
-    land(1, 1, OY, PIECE_OY)
+    weight_tiles(0, 7, 8)
+    far_land(1, 1)
     backward(1, (OO, OY))
     y_leaf(1)
-    land(1, 1, MY, PIECE_MY)
-    land(1, 1, PY, PIECE_PY)
+    side_land(1, 1)
     backward(1, (MY, PY))
     leaves(1)
     near_sum(0)
+    weight_tiles(1, 0, 4)
+    far_sum(1)
     near_free(1)
-    weight_tiles(0, 2)
-    far_sum(1)
+    side_sum(1)
+    weight_tiles(1, 4, 6)
     finish(0)
-    weight_tiles(2, 4)
-    side_sum(1)
     near_sum(1)
-    weight_tiles(4, 8)
+    weight_tiles(1, 6, 8)
     finish(1)
     own_rows = ds(g * SL, SL)
-    back[own_rows, :] = fin[ds(x * SL, SL), :]
-    for slot in range(2):
-        into, outof = tile_copies(slot, 6 + slot)
-        into.wait()
-        outof.wait()
-    for i, (b, k) in enumerate(hops):
-        sender = (h if b == 0 else 1 - h) * 4 + source_x(k)
+    back[own_rows, :] = fin[pl.ds(0, SL), :]
+    for i, hop in enumerate(HOPS):
         remote(
-            fin.at[pl.ds(0, SL)], back.at[ds(sender * SL, SL)], d_send.at[i], d_recv.at[i], (g, to_y)
+            fin.at[pl.ds(0, SL)], back.at[ds(partner(*hop)[0] * SL, SL)], d_send.at[i], d_recv.at[i], (g, to_y)
         ).wait_recv()
     ret_ref[...] = back[...]
     for copy in pending:
@@ -557,16 +593,16 @@
     rows = chosen.shape[1] * chosen.shape[2]
     total = rows * lax.axis_size("fsdp")
     vmem, dma = pltpu.VMEM, pltpu.SemaphoreType.DMA
-    in_vmem, in_hbm = pl.BlockSpec(memory_space=pltpu.VMEM), pl.BlockSpec(memory_space=pl.ANY)
+    in_vmem, in_hbm = pl.BlockSpec(memory_space=pltpu.VMEM), pl.BlockSpec(memory_space=pltpu.HBM)
     return pl.pallas_call(
         layer_kernel,
         out_shape=[
-            jax.ShapeDtypeStruct((rows, width), BF),
-            jax.ShapeDtypeStruct((1, width, hidden), F32),
-            jax.ShapeDtypeStruct((1, hidden, width), F32),
+            vmem((rows, width), BF),
+            vmem((width, hidden), F32),
+            vmem((hidden, width), F32),
         ],
         in_specs=[in_vmem] * 3 + [in_hbm] * 4,
-        out_specs=[in_vmem, in_hbm, in_hbm],
+        out_specs=[in_vmem] * 3,
         scratch_shapes=[
             vmem((rows, width), BF),
             vmem((rows, width), BF),
@@ -584,38 +620,35 @@
             vmem((2, 2, HALF, width), BF),
             vmem((2, 2, CH, width), BF),
             vmem((2, 3, CH, width), BF),
+            vmem((2, 2, QS, width), BF),
             vmem((rows, width), BF),
             vmem((rows, width), BF),
-            vmem((2, 256, hidden), F32),
-            vmem((2, hidden, 256), F32),
             dma((2, 4)),
             dma((2, 7)),
             dma((2, 7)),
             dma((2,)),
             dma((2,)),
-            dma((2, 2, 8)),
-            dma((2, 2, 8)),
+            dma((2, 2, 10)),
+            dma((2, 2, 10)),
             dma((2, 2, 8)),
             dma((2, 2, 8)),
             dma((2, 8)),
             dma((2, 8)),
-            dma((2, 10)),
-            dma((2, 10)),
+            dma((2, 12)),
+            dma((2, 12)),
             dma((7,)),
             dma((7,)),
-            dma((2, 2)),
         ],
         compiler_params=pltpu.CompilerParams(
-            collective_id=0, has_side_effects=True, vmem_limit_bytes=62 * 1024 * 1024
+            collective_id=0, has_side_effects=True, vmem_limit_bytes=LAYER_VMEM
         ),
         name="layer",
     )(chosen, counts, gates, tokens_in, out_grad, w_in, w_out)
 
 
 def shards(tokens_in, out_grad, w_in, w_out, chosen, counts, gates):
-    ret, grad_w_in, grad_w_out = layer(chosen, counts, gates, tokens_in, out_grad, w_in, w_out)
-    grad_in = spread_rows(chosen, ret, tokens_in.shape[0])
-    return (grad_in, grad_w_in, grad_w_out)
+    ret, dwin, dwout = layer(chosen, counts, gates, tokens_in, out_grad, w_in, w_out)
+    return spread_rows(chosen, ret, dwin, dwout, tokens_in.shape[0])
 
 
 def solution(mesh):

time: 134 us -> 122 us (0.910)
  local copies, waits for them, and re-layouts: 6.83 us -> 0.01 us
  Pallas kernels: 125 us -> 119 us
    unnamed x4 -> x2, local copies, waits for them, and re-layouts: 6.83 us -> 0.01 us
    pallas_call x2, Pallas kernels: 125 us -> 119 us  [the longest x1 115 us: layer(): pl.pallas_call(layer_kernel, out_shape=[vmem((rows, width), BF), vmem((wi...]
where the time goes in v3:
time: 122 us; the launch traced here: 120 us
  Pallas kernels  119 us (98%)
    pallas_call x1, Pallas kernels, layer(): pl.pallas_call(layer_kernel, out_shape=[vmem((rows, width), BF), vmem((wi...  115 us
    pallas_call x1, Pallas kernels, spread_rows(): pl.pallas_call(spread_kernel, in_specs=[in_vmem] * 4, out_specs=[in_hbm]...  4.61 us

profile of v3, /device:TPU:4, one launch (start us, length us, event | category | flops | bytes accessed | tf_op | source)
XLA Modules:
  0.0 120.3 jit_solution(10968480800598445028)
XLA Ops:
  0.6 0.0 copy-start
  0.6 114.9 %layer.1 = (bf16[128,2048]{1,0:T(8,128)(2,1)S(1)}, f32[2048,512]{1,0:T(8,128)S(1)}, f32[512,2048]{1,0:T(8,128)S(1)}) custom-call(s32[1,8,16]{2,1,0:T(8,128)} %chosen_ref.3, s32[1,8]{1,0:T(1,128)} %counts_ref.1, f32[1,8,16]{2,1,0:T(8,128)} %gates_ref.1, bf16[1024,2048]{1,0:T(8,128)(2,1)} %tok_hbm.1, bf16[1024,2048]{1,0:T(8,128)(2,1)} %cot_hbm.1, ...), custom_call_target="tpu_custom_call" | custom-call | tf_op jit(solution)/shard_map/layer/pallas_call | solution.py:597
  115.5 0.0 copy-done
  115.5 4.6 %spread_rows.1 = (bf16[1024,2048]{1,0:T(8,128)(2,1)}, f32[1,2048,512]{2,1,0:T(8,128)}, f32[1,512,2048]{2,1,0:T(8,128)}) custom-call(s32[1,8,16]{2,1,0:T(8,128)S(1)} %copy-done, bf16[128,2048]{1,0:T(8,128)(2,1)S(1)} %get-tuple-element.6.ret_ref, f32[2048,512]{1,0:T(8,128)S(1)} %get-tuple-element.7.dwin_ref, f32[512,2048]{1,0:T(8,128)S(1)} %get-tuple-element.8.dwout_ref), custom_call_target="tpu_custom_call" | custom-call | tf_op jit(solution)/shard_map/spread_rows/pallas_call | solution.py:67
Async XLA Ops:
  0.6 114.9 %copy-start = (s32[1,8,16]{2,1,0:T(8,128)S(1)}, s32[1,8,16]{2,1,0:T(8,128)}, u32[]{:S(2)}) copy-start(s32[1,8,16]{2,1,0:T(8,128)} %chosen_ref.3) | copy-start | bytes 1540

commit v4 on v3

--- a/solution.py
+++ b/solution.py
@@ -204,8 +204,6 @@
         pltpu.make_async_copy(win_hbm.at[0], win, w_sem.at[0]),
         pltpu.make_async_copy(wout_hbm.at[0], wout, w_sem.at[1]),
     ]
-    for w in w_copies:
-        w.start()
     barrier = pltpu.get_barrier_semaphore()
     for hop in HOPS:
         pl.semaphore_signal(barrier, inc=1, device_id=partner(*hop), device_id_type=MESH)
@@ -277,6 +275,8 @@
         own_copies.append(own)
     for a in range(2):
         a_start(a, 1)
+    for w in w_copies:
+        w.start()
 
     def ag(a, b, rows, dest, piece):
         return remote(
@@ -562,19 +562,19 @@
     weight_tiles(0, 7, 8)
     far_land(1, 1)
     backward(1, (OO, OY))
+    side_land(1, 1)
     y_leaf(1)
-    side_land(1, 1)
     backward(1, (MY, PY))
+    near_sum(0)
     leaves(1)
-    near_sum(0)
     weight_tiles(1, 0, 4)
     far_sum(1)
     near_free(1)
+    weight_tiles(1, 4, 6)
     side_sum(1)
-    weight_tiles(1, 4, 6)
     finish(0)
+    weight_tiles(1, 6, 8)
     near_sum(1)
-    weight_tiles(1, 6, 8)
     finish(1)
     own_rows = ds(g * SL, SL)
     back[own_rows, :] = fin[pl.ds(0, SL), :]

time: 122 us -> 120 us (0.984)
  Pallas kernels: 119 us -> 117 us
    pallas_call x1, Pallas kernels: 115 us -> 113 us  [layer(): pl.pallas_call(layer_kernel, out_shape=[vmem((rows, width), BF), vmem((wi...]
where the time goes in v4:
time: 120 us; the launch traced here: 118 us
  Pallas kernels  117 us (98%)
    pallas_call x1, Pallas kernels, layer(): pl.pallas_call(layer_kernel, out_shape=[vmem((rows, width), BF), vmem((wi...  113 us
    pallas_call x1, Pallas kernels, spread_rows(): pl.pallas_call(spread_kernel, in_specs=[in_vmem] * 4, out_specs=[in_hbm]...  4.61 us

profile of v4, /device:TPU:4, one launch (start us, length us, event | category | flops | bytes accessed | tf_op | source)
XLA Modules:
  0.0 118.0 jit_solution(18297026145718543177)
XLA Ops:
  0.6 0.0 copy-start
  0.6 112.6 %layer.1 = (bf16[128,2048]{1,0:T(8,128)(2,1)S(1)}, f32[2048,512]{1,0:T(8,128)S(1)}, f32[512,2048]{1,0:T(8,128)S(1)}) custom-call(s32[1,8,16]{2,1,0:T(8,128)} %chosen_ref.3, s32[1,8]{1,0:T(1,128)} %counts_ref.1, f32[1,8,16]{2,1,0:T(8,128)} %gates_ref.1, bf16[1024,2048]{1,0:T(8,128)(2,1)} %tok_hbm.1, bf16[1024,2048]{1,0:T(8,128)(2,1)} %cot_hbm.1, ...), custom_call_target="tpu_custom_call" | custom-call | tf_op jit(solution)/shard_map/layer/pallas_call | solution.py:597
  113.3 0.0 copy-done
  113.3 4.6 %spread_rows.1 = (bf16[1024,2048]{1,0:T(8,128)(2,1)}, f32[1,2048,512]{2,1,0:T(8,128)}, f32[1,512,2048]{2,1,0:T(8,128)}) custom-call(s32[1,8,16]{2,1,0:T(8,128)S(1)} %copy-done, bf16[128,2048]{1,0:T(8,128)(2,1)S(1)} %get-tuple-element.6.ret_ref, f32[2048,512]{1,0:T(8,128)S(1)} %get-tuple-element.7.dwin_ref, f32[512,2048]{1,0:T(8,128)S(1)} %get-tuple-element.8.dwout_ref), custom_call_target="tpu_custom_call" | custom-call | tf_op jit(solution)/shard_map/spread_rows/pallas_call | solution.py:67
Async XLA Ops:
  0.6 112.6 %copy-start = (s32[1,8,16]{2,1,0:T(8,128)S(1)}, s32[1,8,16]{2,1,0:T(8,128)}, u32[]{:S(2)}) copy-start(s32[1,8,16]{2,1,0:T(8,128)} %chosen_ref.3) | copy-start | bytes 1540
